TPU v7x, 32 devices: a whole 2x2x4 slice. The times are simulated.
32 devices in a mesh: dp: 8 (over z, core), expert: 4 (over y, x).
Axes of the slice: x: 2, y: 2, z: 4, core: 2. Of those that a mesh axis runs over, the one named last changes fastest.
Arguments:
- images: bfloat16 [96, 197, 384], P(('dp', 'expert')), may hold values from -6 to 6
- teacher: bfloat16 [96, 197, 384], P(('dp', 'expert')), may hold values from -6 to 6
- out_grad: bfloat16 [96, 197, 384], P(('dp', 'expert')), may hold values from -6 to 6
- valid_mask: int32 [96, 197], P(('dp', 'expert')), may hold values from 0 to 1, as said below
- routes: int32 [96, 197, 2], P(('dp', 'expert')), may hold values from 0 to 7, all different within a row; in each aligned block of 591 rows (0 to 590, 591 to 1181, ..., all dimensions but the last counted through in order) at most 236 rows name the same one
- w_qkv: bfloat16 [384, 1152], P('dp'), may hold values from -0.3125 to 0.3125
- w_out: bfloat16 [384, 384], P('dp'), may hold values from -2 to 2
- gain_attn: bfloat16 [384], P('dp'), may hold values from 0.5 to 1.5
- gain_moe: bfloat16 [384], P('dp'), may hold values from 0.5 to 1.5
- router: bfloat16 [384, 8], P('dp'), may hold values from -0.21875 to 0.21875
- w_in: bfloat16 [8, 384, 1536], P('expert'), may hold values from -0.3125 to 0.3125
- w_back: bfloat16 [8, 1536, 384], P('expert'), may hold values from -0.21875 to 0.21875
Outputs:
- loss: float32 [], replicated
- output: bfloat16 [96, 197, 384], P(('dp', 'expert'))
- grad_images: bfloat16 [96, 197, 384], P(('dp', 'expert'))
- d_w_qkv: float32 [384, 1152], P('dp')
- d_w_out: float32 [384, 384], P('dp')
- d_gain_attn: float32 [384], P('dp')
- d_gain_moe: float32 [384], P('dp')
- d_router: float32 [384, 8], P('dp')
- d_w_in: float32 [8, 384, 1536], P('expert', 'dp')
- d_w_back: float32 [8, 1536, 384], P('expert', 'dp')
Inputs may be any that keep to these rules, and one draw needn't show every extreme that they name: `routes`: the 2 experts of a token differ. Among the tokens of one device no expert is named more than 236 times. `valid_mask`: the first token of every image is valid.
All inputs are finite; a program needn't handle non-finite values.
Results may differ from a plain program's by a relative error of at most 0.013.
Values may be sent and summed in bfloat16 or wider, within the bound.
A program may use at most 192 MiB of HBM per device.

v0:
```python
import jax
import jax.numpy as jnp
from jax import lax
from jax.sharding import PartitionSpec as P

HEAD_DIM = 64
TOP = 2


def layer_norm(values, gain):
    middle = jnp.mean(values, axis=-1, keepdims=True)
    center = values - middle
    variance = jnp.mean(center * center, axis=-1, keepdims=True)
    return center * lax.rsqrt(variance + 1e-06) * gain


def gelu_exact(values):
    return jax.nn.gelu(values, approximate=False)


def take_rows(table, index):
    padded = jnp.concatenate([table, jnp.zeros((1, table.shape[1]), table.dtype)], axis=0)
    return jnp.take(padded, index, axis=0)


def slot_tables(route_rows, experts, capacity):
    flat = route_rows.reshape(-1)
    pairs = flat.shape[0]
    hits = (flat[:, None] == jnp.arange(experts, dtype=jnp.int32)[None, :]).astype(jnp.int32)
    order = jnp.sum((jnp.cumsum(hits, axis=0) - 1) * hits, axis=1)
    slot = flat * capacity + order
    owner = (
        jnp.full((experts * capacity,), pairs, jnp.int32)
        .at[slot]
        .set(jnp.arange(pairs, dtype=jnp.int32))
    )
    return (slot, owner)


def body(
    images,
    teacher,
    out_grad,
    valid_mask,
    routes,
    w_qkv,
    w_out,
    gain_attn,
    gain_moe,
    router,
    w_in,
    w_back,
):
    img_count, seq_len, width = images.shape
    rows = img_count * seq_len
    exp_local = w_in.shape[0]
    owners = lax.axis_size("expert")
    experts = exp_local * owners
    heads = width // HEAD_DIM
    capacity = max(2, rows * 16 // (experts * 5))
    total_rows = rows * lax.axis_size("dp") * owners
    scale = HEAD_DIM ** (-0.5)
    mask_f = valid_mask.reshape(rows).astype(jnp.float32)
    local_count = jnp.sum(mask_f)
    full_qkv, full_out, gain_one, gain_two, full_router = (
        lax.all_gather(w_qkv, "dp", axis=0, tiled=True),
        lax.all_gather(w_out, "dp", axis=0, tiled=True),
        lax.all_gather(gain_attn, "dp", axis=0, tiled=True),
        lax.all_gather(gain_moe, "dp", axis=0, tiled=True),
        lax.all_gather(router, "dp", axis=0, tiled=True),
    )
    gain_first = gain_one.astype(jnp.float32)
    gain_second = gain_two.astype(jnp.float32)
    inputs = images.astype(jnp.float32)
    normed_one = layer_norm(inputs, gain_first).astype(jnp.bfloat16)
    projected = jnp.einsum(
        "isd,de->ise", normed_one, full_qkv, preferred_element_type=jnp.float32
    ).astype(jnp.bfloat16)
    projected = projected.reshape(img_count, seq_len, 3, heads, HEAD_DIM)
    query = projected[:, :, 0]
    keys = projected[:, :, 1]
    values = projected[:, :, 2]
    scores = jnp.einsum("iqhd,ikhd->ihqk", query, keys, preferred_element_type=jnp.float32) * scale
    row_top = jnp.max(scores, axis=-1, keepdims=True)
    shifted = jnp.exp(scores - row_top)
    row_total = jnp.sum(shifted, axis=-1, keepdims=True)
    probs = shifted / row_total
    log_total = row_top + jnp.log(row_total)
    mixed = jnp.einsum(
        "ihqk,ikhd->iqhd", probs.astype(jnp.bfloat16), values, preferred_element_type=jnp.float32
    )
    mixed = mixed.astype(jnp.bfloat16).reshape(img_count, seq_len, width)
    attn = jnp.einsum("isd,de->ise", mixed, full_out, preferred_element_type=jnp.float32)
    hidden_one = inputs + attn
    normed_two = layer_norm(hidden_one, gain_second).astype(jnp.bfloat16).reshape(rows, width)
    logits = jnp.dot(normed_two, full_router, preferred_element_type=jnp.float32)
    route_rows = routes.reshape(rows, TOP)

    def gate_fn(scores_in):
        chances = jax.nn.softmax(scores_in, axis=-1)
        chosen = jnp.take_along_axis(chances, route_rows, axis=1)
        return chosen / jnp.sum(chosen, axis=1, keepdims=True)

    gates, gate_back = jax.vjp(gate_fn, logits)
    slot, owner = slot_tables(route_rows, experts, capacity)
    token_of = jnp.where(owner < rows * TOP, owner // TOP, rows)
    outgoing = take_rows(normed_two, token_of).reshape(owners, exp_local, capacity, width)
    arrived = lax.all_to_all(outgoing, "expert", split_axis=0, concat_axis=0, tiled=True)
    expert_pre = jnp.einsum("secd,edf->secf", arrived, w_in, preferred_element_type=jnp.float32)
    activated = gelu_exact(expert_pre).astype(jnp.bfloat16)
    made = jnp.einsum(
        "secf,efd->secd", activated, w_back, preferred_element_type=jnp.float32
    ).astype(jnp.bfloat16)
    returned = lax.all_to_all(made, "expert", split_axis=0, concat_axis=0, tiled=True).reshape(
        experts * capacity, width
    )
    picked = jnp.take(returned, slot, axis=0).reshape(rows, TOP, width).astype(jnp.float32)
    mixture = jnp.sum(gates[:, :, None] * picked, axis=1)
    combined = hidden_one.reshape(rows, width) + mixture
    diff = combined - teacher.reshape(rows, width).astype(jnp.float32)
    local_sq = jnp.sum(mask_f[:, None] * diff * diff)
    count, sq_total = lax.psum((local_count, local_sq), ("dp", "expert"))
    loss = sq_total / (count * width)
    grad_out = (
        out_grad.reshape(rows, width).astype(jnp.float32)
        + total_rows / count * mask_f[:, None] * diff
    )
    grad_picked = (
        (gates[:, :, None] * grad_out[:, None, :]).astype(jnp.bfloat16).reshape(rows * TOP, width)
    )
    grad_gates = jnp.sum(picked * grad_out[:, None, :], axis=2)
    grad_logits = gate_back(grad_gates)[0].astype(jnp.bfloat16)
    grad_outgoing = take_rows(grad_picked, owner).reshape(owners, exp_local, capacity, width)
    grad_arrived = lax.all_to_all(grad_outgoing, "expert", split_axis=0, concat_axis=0, tiled=True)
    inputs_again = lax.all_to_all(outgoing, "expert", split_axis=0, concat_axis=0, tiled=True)
    pre_again = jnp.einsum("secd,edf->secf", inputs_again, w_in, preferred_element_type=jnp.float32)
    act_again = gelu_exact(pre_again).astype(jnp.bfloat16)
    grad_act = jnp.einsum(
        "secd,efd->secf", grad_arrived, w_back, preferred_element_type=jnp.float32
    )
    gelu_back = jax.vjp(gelu_exact, pre_again)[1]
    grad_pre = gelu_back(grad_act)[0].astype(jnp.bfloat16)
    d_back_part = jnp.einsum(
        "secf,secd->efd", act_again, grad_arrived, preferred_element_type=jnp.float32
    )
    d_in_part = jnp.einsum(
        "secd,secf->edf", inputs_again, grad_pre, preferred_element_type=jnp.float32
    )
    grad_sent = jnp.einsum(
        "secf,edf->secd", grad_pre, w_in, preferred_element_type=jnp.float32
    ).astype(jnp.bfloat16)
    grad_home = lax.all_to_all(
        grad_sent, "expert", split_axis=0, concat_axis=0, tiled=True
    ).reshape(experts * capacity, width)
    grad_two = jnp.sum(
        jnp.take(grad_home, slot, axis=0).reshape(rows, TOP, width).astype(jnp.float32), axis=1
    )
    grad_two = grad_two + jnp.einsum(
        "te,de->td", grad_logits, full_router, preferred_element_type=jnp.float32
    )
    d_router_part = jnp.einsum(
        "td,te->de", normed_two, grad_logits, preferred_element_type=jnp.float32
    )
    norm_two_back = jax.vjp(layer_norm, hidden_one, gain_second)[1]
    grad_hidden_part, d_gain_two_part = norm_two_back(grad_two.reshape(img_count, seq_len, width))
    grad_hidden = grad_out.reshape(img_count, seq_len, width) + grad_hidden_part
    grad_attn = grad_hidden.astype(jnp.bfloat16)
    d_out_part = jnp.einsum("isd,ise->de", mixed, grad_attn, preferred_element_type=jnp.float32)
    grad_mixed = jnp.einsum("ise,de->isd", grad_attn, full_out, preferred_element_type=jnp.float32)
    grad_mixed = grad_mixed.astype(jnp.bfloat16).reshape(img_count, seq_len, heads, HEAD_DIM)
    scores_again = (
        jnp.einsum("iqhd,ikhd->ihqk", query, keys, preferred_element_type=jnp.float32) * scale
    )
    probs_again = jnp.exp(scores_again - log_total)
    grad_values = jnp.einsum(
        "ihqk,iqhd->ikhd",
        probs_again.astype(jnp.bfloat16),
        grad_mixed,
        preferred_element_type=jnp.float32,
    )
    grad_probs = jnp.einsum(
        "iqhd,ikhd->ihqk", grad_mixed, values, preferred_element_type=jnp.float32
    )
    grad_scores = probs_again * (
        grad_probs - jnp.sum(grad_probs * probs_again, axis=-1, keepdims=True)
    )
    grad_scores = grad_scores.astype(jnp.bfloat16)
    grad_query = (
        jnp.einsum("ihqk,ikhd->iqhd", grad_scores, keys, preferred_element_type=jnp.float32) * scale
    )
    grad_keys = (
        jnp.einsum("ihqk,iqhd->ikhd", grad_scores, query, preferred_element_type=jnp.float32)
        * scale
    )
    grad_projected = jnp.stack([grad_query, grad_keys, grad_values], axis=2).astype(jnp.bfloat16)
    grad_projected = grad_projected.reshape(img_count, seq_len, 3 * width)
    d_qkv_part = jnp.einsum(
        "isd,ise->de", normed_one, grad_projected, preferred_element_type=jnp.float32
    )
    grad_one = jnp.einsum(
        "ise,de->isd", grad_projected, full_qkv, preferred_element_type=jnp.float32
    )
    norm_one_back = jax.vjp(layer_norm, inputs, gain_first)[1]
    grad_input_part, d_gain_one_part = norm_one_back(grad_one)
    grad_images = (grad_hidden + grad_input_part).astype(jnp.bfloat16)
    shards = (
        lax.psum_scatter(
            d_qkv_part.astype(jnp.bfloat16), "dp", scatter_dimension=0, tiled=True
        ).astype(jnp.float32),
        lax.psum_scatter(
            d_out_part.astype(jnp.bfloat16), "dp", scatter_dimension=0, tiled=True
        ).astype(jnp.float32),
        lax.psum_scatter(
            d_gain_one_part.astype(jnp.bfloat16), "dp", scatter_dimension=0, tiled=True
        ).astype(jnp.float32),
        lax.psum_scatter(
            d_gain_two_part.astype(jnp.bfloat16), "dp", scatter_dimension=0, tiled=True
        ).astype(jnp.float32),
        lax.psum_scatter(
            d_router_part.astype(jnp.bfloat16), "dp", scatter_dimension=0, tiled=True
        ).astype(jnp.float32),
        lax.psum_scatter(
            d_in_part.astype(jnp.bfloat16), "dp", scatter_dimension=1, tiled=True
        ).astype(jnp.float32),
        lax.psum_scatter(
            d_back_part.astype(jnp.bfloat16), "dp", scatter_dimension=1, tiled=True
        ).astype(jnp.float32),
    )
    dense = (shards[0], shards[1], shards[2], shards[3], shards[4])
    d_in_total = shards[5]
    d_back_total = shards[6]
    summed = (
        lax.psum(dense[0].astype(jnp.bfloat16), "expert").astype(jnp.float32),
        lax.psum(dense[1].astype(jnp.bfloat16), "expert").astype(jnp.float32),
        lax.psum(dense[2].astype(jnp.bfloat16), "expert").astype(jnp.float32),
        lax.psum(dense[3].astype(jnp.bfloat16), "expert").astype(jnp.float32),
        lax.psum(dense[4].astype(jnp.bfloat16), "expert").astype(jnp.float32),
    )
    output = combined.astype(jnp.bfloat16).reshape(img_count, seq_len, width)
    return (
        loss,
        output,
        grad_images,
        summed[0],
        summed[1],
        summed[2],
        summed[3],
        summed[4],
        d_in_total,
        d_back_total,
    )


def solution(mesh):
    in_specs = (
        P(("dp", "expert"), None, None),
        P(("dp", "expert"), None, None),
        P(("dp", "expert"), None, None),
        P(("dp", "expert"), None),
        P(("dp", "expert"), None, None),
        P("dp", None),
        P("dp", None),
        P("dp"),
        P("dp"),
        P("dp", None),
        P("expert", None, None),
        P("expert", None, None),
    )
    out_specs = (
        P(),
        P(("dp", "expert"), None, None),
        P(("dp", "expert"), None, None),
        P("dp", None),
        P("dp", None),
        P("dp"),
        P("dp"),
        P("dp", None),
        P("expert", "dp", None),
        P("expert", "dp", None),
    )
    return jax.shard_map(body, mesh=mesh, in_specs=in_specs, out_specs=out_specs, check_vma=False)
```

profile of v0, /device:TPU:0, one launch (start us, length us, event | category | flops | bytes accessed | tf_op | source)
XLA Modules:
  0.0 623.9 jit_solution(1569113898963617501)
XLA Ops:
  12.6 18.1 %all-reduce.8 = (bf16[384]{0:T(512)(128)(2,1)S(1)}, bf16[384]{0:T(512)(128)(2,1)S(1)}) all-reduce(bf16[384]{0:T(512)(128)(2,1)S(1)} %dynamic-update-slice, bf16[384]{0:T(512)(128)(2,1)S(1)} %dynamic-update-slice.1), channel_id=1, replica_groups=mesh['dp'=8,'expert'=4] {'dp'}, use_global_device_ids=true, to_apply=%add.3 | all-reduce | flops 768 | bytes 3072
  33.9 16.0 %all_gather.16 = bf16[384,1152]{1,0:T(8,128)(2,1)S(1)} all-gather(bf16[48,1152]{1,0:T(8,128)(2,1)} %param.19), channel_id=1, replica_groups=mesh['dp'=8,'expert'=4] {'dp'}, dimensions={0}, use_global_device_ids=true | all-gather | bytes 995328 | tf_op jit(solution)/shard_map/all_gather | solution.py:66
  50.8 3.1 convolution_convert_fusion
  54.0 3.6 copy.114
  60.3 2.6 fusion.55
  63.0 14.2 %all_gather.17 = bf16[384,384]{1,0:T(8,128)(2,1)S(1)} all-gather(bf16[48,384]{1,0:T(8,128)(2,1)S(1)} %copy-done.63), channel_id=1, replica_groups=mesh['dp'=8,'expert'=4] {'dp'}, dimensions={0}, use_global_device_ids=true | all-gather | bytes 331776 | tf_op jit(solution)/shard_map/all_gather | solution.py:67
  85.8 6.4 %scatter_custom_fusion = s32[1888]{0:T(1024)S(1)} fusion(s32[1182]{0:T(1024)S(1)} %fusion.101, s32[1182]{0:T(1024)S(1)} %iota.8, s32[]{:T(128)} %constant.70.clone.1), kind=kCustom, calls=%fused_computation.188 | custom fusion | bytes 7556 | tf_op jit(solution)/shard_map/scatter | solution.py:35
  92.9 6.6 %gather_fusion = bf16[1888,384]{1,0:T(8,128)(2,1)} fusion(bf16[592,384]{1,0:T(8,128)(2,1)S(1)} %concatenate.6, s32[2048]{0:T(1024)S(1)} %pad_clamp_fusion.2), kind=kCustom, calls=%fused_computation.2 | custom fusion | bytes 2907520 | tf_op jit(solution)/shard_map/jit(_take)/gather | solution.py:23
  106.0 4.4 all-to-all-start
  110.4 13.0 %all-gather = bf16[8,48,8]{1,2,0:T(8,128)(2,1)S(1)} all-gather(bf16[1,48,8]{1,2,0:T(8,128)(2,1)S(1)} %bitcast.240), channel_id=1, replica_groups=mesh['dp'=8,'expert'=4] {'dp'}, dimensions={0}, use_global_device_ids=true | all-gather | bytes 6912 | tf_op jit(solution)/shard_map/all_gather | solution.py:70
  124.2 39.4 %psum.50 = f32[]{:T(128)} all-reduce(f32[]{:T(128)} %convert_reduce_fusion.1), channel_id=1, replica_groups=mesh['dp'=8,'expert'=4] {'dp','expert'}, use_global_device_ids=true, to_apply=%region_17.19 | all-reduce | flops 1 | bytes 8 | tf_op jit(solution)/shard_map/psum | solution.py:122
  166.0 11.7 %gather_fusion.2 = f32[1182]{0:T(1024)S(1)} fusion(f32[591,8]{0,1:T(8,128)S(1)} %fusion.93, s32[1182]{0:T(1024)S(1)} %reshape.419), kind=kCustom, calls=%fused_computation.4 | custom fusion | bytes 18912 | tf_op jit(solution)/shard_map/jvp(jit(take_along_axis))/gather | solution.py:101
  185.1 30.4 %fusion.9 = (bf16[4,2,236,1536]{3,2,0,1:T(8,128)(2,1)S(1)}, f32[4,2,236,1536]{3,2,0,1:T(8,128)}, f32[2,4,236,1536]{3,2,1,0:T(8,128)}) fusion(bf16[2,384,1536]{2,1,0:T(8,128)(2,1)S(1)} %copy-done, bf16[4,2,236,384]{3,1,2,0:T(2,128)(2,1)} %all-to-all-done), kind=kOutput, calls=%fused_computation.24 | convolution fusion | flops 2415673344 | bytes 32808960 | tf_op jit(solution)/shard_map/secd,edf->secf/dot_general | solution.py:109
  215.6 3.2 fusion.46
  218.9 2.6 copy.132
  221.5 4.7 all-to-all-start.1
  228.6 15.2 %all-to-all-done.1 = bf16[4,2,236,384]{3,1,2,0:T(2,128)(2,1)} async-done(((bf16[4,2,236,384]{3,1,2,0:T(2,128)(2,1)}), bf16[4,2,236,384]{3,1,2,0:T(2,128)(2,1)}, u32[]{:S(2)}, u32[]{:S(2)}) %all-to-all-start.1) | async-done | bytes 1450016 | tf_op jit(solution)/shard_map/all_to_all | solution.py:114
  243.8 2.7 copy.133
  248.9 5.6 gather_fusion.3
  255.9 3.2 reshape.383
  259.2 9.5 %multiply_reduce_fusion.3 = f32[591,384]{1,0:T(8,128)S(1)} fusion(f32[591,2,384]{2,1,0:T(2,128)} %reshape.383, f32[591,2]{1,0:T(8,128)} %copy.126), kind=kLoop, calls=%fused_computation.64 | loop fusion | flops 680832 | bytes 2728056 | tf_op jit(solution)/shard_map/reduce_sum | solution.py:118
  273.5 3.4 mul.359
  279.2 6.6 %gather_fusion.1 = bf16[1888,384]{1,0:T(8,128)(2,1)} fusion(bf16[1183,384]{1,0:T(8,128)(2,1)S(1)} %concatenate.7, s32[2048]{0:T(1024)S(1)} %pad_clamp_fusion), kind=kCustom, calls=%fused_computation.3 | custom fusion | bytes 2907520 | tf_op jit(solution)/shard_map/jit(_take)/gather | solution.py:23
  292.4 4.3 all-to-all-start.2
  297.3 16.9 %all-to-all-done.2 = bf16[4,2,236,384]{3,1,2,0:T(2,128)(2,1)} async-done(((bf16[4,2,236,384]{3,1,2,0:T(2,128)(2,1)}), bf16[4,2,236,384]{3,1,2,0:T(2,128)(2,1)}, u32[]{:S(2)}, u32[]{:S(2)}) %all-to-all-start.2) | async-done | bytes 1450016 | tf_op jit(solution)/shard_map/all_to_all | solution.py:134
  314.3 12.1 %fusion.6 = bf16[4,2,236,1536]{3,2,0,1:T(8,128)(2,1)S(1)} fusion(f32[4,2,236,1536]{3,2,0,1:T(8,128)} %get-tuple-element.27, f32[2,4,236,1536]{3,2,1,0:T(8,128)} %get-tuple-element.43, bf16[2,1536,384]{2,1,0:T(8,128)(2,1)} %param.25, bf16[4,2,236,384]{3,1,2,0:T(2,128)(2,1)} %all-to-all-done.2), kind=kOutput, calls=%fused_computation.16 | convolution fusion | flops 2267774976 | bytes 32808960 | tf_op jit(solution)/shard_map/secd,efd->secf/dot_general | solution.py:138
  326.3 3.2 fusion.43
  329.6 2.6 copy.137
  332.2 4.5 all-to-all-start.3
  338.7 7.3 %scatter_custom_fusion.1 = f32[4728]{0:T(1024)S(1)} fusion(s32[1182]{0:T(1024)S(1)} %reshape.433, f32[1182]{0:T(1024)S(1)} %reshape.435, f32[]{:T(128)} %constant.40.clone.1), kind=kCustom, calls=%fused_computation.162 | custom fusion | flops 1182 | bytes 18916
  346.1 8.1 %all-to-all-done.3 = bf16[4,2,236,384]{3,1,2,0:T(2,128)(2,1)} async-done(((bf16[4,2,236,384]{3,1,2,0:T(2,128)(2,1)}), bf16[4,2,236,384]{3,1,2,0:T(2,128)(2,1)}, u32[]{:S(2)}, u32[]{:S(2)}) %all-to-all-start.3) | async-done | bytes 1450016 | tf_op jit(solution)/shard_map/all_to_all | solution.py:152
  354.2 2.7 copy.138
  356.9 2.6 reshape.375
  359.5 5.6 gather_fusion.4
  366.6 3.3 reshape.386
  369.9 4.7 reduce_sum.225
  381.0 3.0 multiply_reduce_fusion.4
  387.1 3.5 multiply_reduce_fusion
  402.6 26.8 %reduce-scatter.8.cloned.1.call-done = bf16[48,1152]{1,0:T(8,128)(2,1)} async-done(((bf16[384,1152]{1,0:T(8,128)(2,1)}), bf16[48,1152]{1,0:T(8,128)(2,1)}) %reduce-scatter.8.cloned.1.call-update) | async-done | bytes 110608 | tf_op jit(solution)/shard_map/reduce_scatter | solution.py:207
  429.7 8.1 %bitcast_convert_fusion = bf16[2,1536,384]{2,1,0:T(8,128)(2,1)} fusion(bf16[4,2,236,1536]{3,2,0,1:T(8,128)(2,1)} %copy-done.71, bf16[4,2,236,384]{3,1,2,0:T(2,128)(2,1)} %all-to-all-done.2), kind=kOutput, calls=%fused_computation.38 | convolution fusion | flops 2228355072 | bytes 9609216 | tf_op jit(solution)/shard_map/secf,secd->efd/dot_general | solution.py:143
  437.8 7.3 %bitcast_convert_fusion.1 = bf16[2,384,1536]{2,1,0:T(8,128)(2,1)} fusion(bf16[4,2,236,1536]{3,2,0,1:T(8,128)(2,1)} %copy-done.72, bf16[4,2,236,384]{3,1,2,0:T(2,128)(2,1)} %all-to-all-done), kind=kOutput, calls=%fused_computation.39 | convolution fusion | flops 2228355072 | bytes 9609216 | tf_op jit(solution)/shard_map/secd,secf->edf/dot_general | solution.py:146
  446.4 14.6 %reduce-scatter.16.cloned.1.call-done = bf16[48,8]{1,0:T(8,128)(2,1)} async-done(((bf16[384,8]{1,0:T(8,128)(2,1)}), bf16[48,8]{1,0:T(8,128)(2,1)}) %reduce-scatter.16.cloned.1.call-update) | async-done | bytes 784
  461.8 38.1 %psum.49 = f32[]{:T(128)} all-reduce(f32[]{:T(128)} %get-tuple-element.15), channel_id=1, replica_groups=mesh['dp'=8,'expert'=4] {'dp','expert'}, use_global_device_ids=true, to_apply=%region_15.17 | all-reduce | flops 1 | bytes 8 | tf_op jit(solution)/shard_map/psum | solution.py:122
  499.9 3.1 fusion.74
  503.9 14.6 %all-reduce.7 = (bf16[384]{0:T(512)(128)(2,1)S(1)}, bf16[384]{0:T(512)(128)(2,1)S(1)}) all-reduce(bf16[384]{0:T(512)(128)(2,1)S(1)} %get-tuple-element.13, bf16[384]{0:T(512)(128)(2,1)S(1)} %get-tuple-element.11), channel_id=4, replica_groups=mesh['dp'=8,'expert'=4] {'dp'}, use_global_device_ids=true, to_apply=%region_33.35.clone | all-reduce | flops 768 | bytes 3072
  521.9 17.0 %all-reduce.9 = (bf16[48,384]{1,0:T(8,128)(2,1)S(1)}, bf16[48]{0:T(256)(128)(2,1)S(1)}, bf16[48]{0:T(256)(128)(2,1)S(1)}, bf16[48,8]{0,1:T(8,128)(2,1)S(1)}) all-reduce(bf16[48,384]{1,0:T(8,128)(2,1)} %reduce-scatter.10.cloned.1.call-done, bf16[48]{0:T(256)(128)(2,1)S(1)} %dynamic-slice.3, ...), channel_id=1, replica_groups=mesh['dp'=8,'expert'=4] {'expert'}, use_global_device_ids=true, to_apply=%region_31.33 | all-reduce | flops 18912 | bytes 75648 | tf_op jit(solution)/shard_map/psum | solution.py:234
  542.8 32.7 %reduce-scatter.14.cloned.1.call-done = bf16[2,192,384]{2,1,0:T(8,128)(2,1)} async-done(((bf16[2,1536,384]{2,1,0:T(8,128)(2,1)}), bf16[2,192,384]{2,1,0:T(8,128)(2,1)}) %reduce-scatter.14.cloned.1.call-update) | async-done | bytes 294928 | tf_op jit(solution)/shard_map/reduce_scatter | solution.py:225
  577.3 36.4 %reduce-scatter.12.cloned.1.call-done = bf16[2,48,1536]{2,1,0:T(8,128)(2,1)} async-done(((bf16[2,384,1536]{2,1,0:T(8,128)(2,1)}), bf16[2,48,1536]{2,1,0:T(8,128)(2,1)}) %reduce-scatter.12.cloned.1.call-update) | async-done | bytes 294928 | tf_op jit(solution)/shard_map/reduce_scatter | solution.py:222
  (300 shorter events, 94.2 us)
Async XLA Ops:
  7.2 177.9 %copy-start = (bf16[2,384,1536]{2,1,0:T(8,128)(2,1)S(1)}, bf16[2,384,1536]{2,1,0:T(8,128)(2,1)}, u32[]{:S(2)}) copy-start(bf16[2,384,1536]{2,1,0:T(8,128)(2,1)} %param.24) | copy-start | bytes 7077892
  30.7 26.9 %copy-start.64 = (f32[384]{0:T(512)}, f32[384]{0:T(512)S(1)}, u32[]{:S(2)}) copy-start(f32[384]{0:T(512)S(1)} %convert_element_type.188) | copy-start | bytes 4612
  31.9 18.0 %copy-start.44 = (f32[3,197]{1,0:T(4,128)}, f32[3,197]{1,0:T(4,128)S(1)}, u32[]{:S(2)}) copy-start(f32[3,197]{1,0:T(4,128)S(1)} %broadcast_multiply_fusion.3) | copy-start | bytes 7096
  33.9 16.1 %copy-start.55 = (f32[3,197]{1,0:T(4,128)}, f32[3,197]{1,0:T(4,128)S(1)}, u32[]{:S(2)}) copy-start(f32[3,197]{1,0:T(4,128)S(1)} %fusion.104) | copy-start | bytes 7096
  60.3 16.9 %copy-start.10 = (bf16[3,197,384]{2,1,0:T(8,128)(2,1)S(1)}, bf16[3,197,384]{2,1,0:T(8,128)(2,1)}, u32[]{:S(2)}) copy-start(bf16[3,197,384]{2,1,0:T(8,128)(2,1)} %param.14) | copy-start | bytes 1361668
  63.0 15.9 %copy-start.22 = (bf16[3,6,64,197]{3,2,1,0:T(8,128)(2,1)}, bf16[3,6,64,197]{3,2,1,0:T(8,128)(2,1)S(1)}, u32[]{:S(2)}) copy-start(bf16[3,6,64,197]{3,2,1,0:T(8,128)(2,1)S(1)} %fusion.55) | copy-start | bytes 1361668
  82.2 82.4 %copy-start.16 = (bf16[591,384]{1,0:T(8,128)(2,1)}, bf16[591,384]{1,0:T(8,128)(2,1)S(1)}, u32[]{:S(2)}) copy-start(bf16[591,384]{1,0:T(8,128)(2,1)S(1)} %reshape.369) | copy-start | bytes 1361668
  82.4 10.4 %copy-start.31 = (s32[1182]{0:T(1024)}, s32[1182]{0:T(1024)S(1)}, u32[]{:S(2)}) copy-start(s32[1182]{0:T(1024)S(1)} %eq.22) | copy-start | bytes 14188
  85.3 7.5 %copy-start.40 = (s32[1182]{0:T(1024)}, s32[1182]{0:T(1024)S(1)}, u32[]{:S(2)}) copy-start(s32[1182]{0:T(1024)S(1)} %fusion.90) | copy-start | bytes 14188
  102.0 8.3 %copy-start.39 = (s32[3,197,2]{1,2,0:T(2,128)S(1)}, s32[3,197,2]{1,2,0:T(2,128)}, u32[]{:S(2)}) copy-start(s32[3,197,2]{1,2,0:T(2,128)} %param.18) | copy-start | bytes 14188
  102.0 8.4 %copy-start.67 = (bf16[48,8]{0,1:T(8,128)(2,1)S(1)}, bf16[48,8]{0,1:T(8,128)(2,1)}, u32[]{:S(2)}) copy-start(bf16[48,8]{0,1:T(8,128)(2,1)} %param.23) | copy-start | bytes 2308
  103.7 19.7 %copy-start.61 = (s32[3,197]{1,0:T(4,128)S(1)}, s32[3,197]{1,0:T(4,128)}, u32[]{:S(2)}) copy-start(s32[3,197]{1,0:T(4,128)} %param.17) | copy-start | bytes 7096
  106.0 79.1 %all-to-all-start = ((bf16[4,2,236,384]{3,1,2,0:T(2,128)(2,1)}), bf16[4,2,236,384]{3,1,2,0:T(2,128)(2,1)}, u32[]{:S(2)}, u32[]{:S(2)}) async-start(bf16[4,2,236,384]{3,1,2,0:T(2,128)(2,1)} %copy.130), calls=%async_computation | async-start | bytes 2899968 | tf_op jit(solution)/shard_map/all_to_all | solution.py:108
  123.5 41.3 %copy-start.50 = (bf16[384,8]{0,1:T(8,128)(2,1)}, bf16[384,8]{0,1:T(8,128)(2,1)S(1)}, u32[]{:S(2)}) copy-start(bf16[384,8]{0,1:T(8,128)(2,1)S(1)} %reshape.452) | copy-start | bytes 18436
  166.0 13.7 %copy-start.4 = (f32[3,197,384]{2,1,0:T(8,128)S(1)}, f32[3,197,384]{2,1,0:T(8,128)}, u32[]{:S(2)}) copy-start(f32[3,197,384]{2,1,0:T(8,128)} %copy-done.3) | copy-start | bytes 2723332
  185.1 30.5 %copy-start.70 = (bf16[2,1536,384]{2,1,0:T(8,128)(2,1)S(1)}, bf16[2,1536,384]{2,1,0:T(8,128)(2,1)}, u32[]{:S(2)}) copy-start(bf16[2,1536,384]{2,1,0:T(8,128)(2,1)} %param.25) | copy-start | bytes 7077892
  218.8 7.4 %copy-start.62 = (s32[3,197]{1,0:T(4,128)S(1)}, s32[3,197]{1,0:T(4,128)}, u32[]{:S(2)}) copy-start(s32[3,197]{1,0:T(4,128)} %param.17) | copy-start | bytes 7096
  218.8 7.5 %copy-start.23 = (bf16[3,197,384]{2,1,0:T(8,128)(2,1)S(1)}, bf16[3,197,384]{2,1,0:T(8,128)(2,1)}, u32[]{:S(2)}) copy-start(bf16[3,197,384]{2,1,0:T(8,128)(2,1)} %param.16) | copy-start | bytes 1361668
  218.8 8.6 %copy-start.17 = (bf16[3,197,384]{2,1,0:T(8,128)(2,1)S(1)}, bf16[3,197,384]{2,1,0:T(8,128)(2,1)}, u32[]{:S(2)}) copy-start(bf16[3,197,384]{2,1,0:T(8,128)(2,1)} %param.15) | copy-start | bytes 1361668
  218.8 9.6 %copy-start.66 = (pred[1888]{0:T(1024)(128)(4,1)S(1)}, pred[1888]{0:T(1024)(128)(4,1)}, u32[]{:S(2)}) copy-start(pred[1888]{0:T(1024)(128)(4,1)} %get-tuple-element.34) | copy-start | bytes 5668
  218.8 9.7 %copy-start.32 = (s32[1182]{0:T(1024)S(1)}, s32[1182]{0:T(1024)}, u32[]{:S(2)}) copy-start(s32[1182]{0:T(1024)} %copy-done.31) | copy-start | bytes 14188
  218.8 9.7 %copy-start.41 = (s32[1182]{0:T(1024)S(1)}, s32[1182]{0:T(1024)}, u32[]{:S(2)}) copy-start(s32[1182]{0:T(1024)} %copy-done.40) | copy-start | bytes 14188
  218.9 9.7 %copy-start.43 = (s32[1888]{0:T(1024)S(1)}, s32[1888]{0:T(1024)}, u32[]{:S(2)}) copy-start(s32[1888]{0:T(1024)} %copy-done.42) | copy-start | bytes 22660
  221.5 22.4 %all-to-all-start.1 = ((bf16[4,2,236,384]{3,1,2,0:T(2,128)(2,1)}), bf16[4,2,236,384]{3,1,2,0:T(2,128)(2,1)}, u32[]{:S(2)}, u32[]{:S(2)}) async-start(bf16[4,2,236,384]{3,1,2,0:T(2,128)(2,1)} %copy.132), calls=%async_computation.1 | async-start | bytes 2899968 | tf_op jit(solution)/shard_map/all_to_all | solution.py:114
  288.4 8.3 %copy-start.54 = (s32[591,2,1]{0,1,2:T(2,128)S(1)}, s32[591,2,1]{0,1,2:T(2,128)}, u32[]{:S(2)}) copy-start(s32[591,2,1]{0,1,2:T(2,128)} %get-tuple-element.35) | copy-start | bytes 14188
  288.4 8.3 %copy-start.68 = (s32[2]{0:T(128)S(1)}, s32[2]{0:T(128)}, u32[]{:S(2)}) copy-start(s32[2]{0:T(128)} %constant.189) | copy-start | bytes 28
  288.4 8.4 %copy-start.69 = (s32[2]{0:T(128)S(1)}, s32[2]{0:T(128)}, u32[]{:S(2)}) copy-start(s32[2]{0:T(128)} %constant.192) | copy-start | bytes 28
  292.4 21.9 %all-to-all-start.2 = ((bf16[4,2,236,384]{3,1,2,0:T(2,128)(2,1)}), bf16[4,2,236,384]{3,1,2,0:T(2,128)(2,1)}, u32[]{:S(2)}, u32[]{:S(2)}) async-start(bf16[4,2,236,384]{3,1,2,0:T(2,128)(2,1)} %copy.135), calls=%async_computation.2 | async-start | bytes 2899968 | tf_op jit(solution)/shard_map/all_to_all | solution.py:134
  329.6 7.2 %copy-start.47 = (f32[591]{0:T(1024)S(1)}, f32[591]{0:T(1024)}, u32[]{:S(2)}) copy-start(f32[591]{0:T(1024)} %copy-done.46) | copy-start | bytes 7096
  329.6 7.2 %copy-start.30 = (f32[3,6,197]{2,1,0:T(8,128)S(1)}, f32[3,6,197]{2,1,0:T(8,128)}, u32[]{:S(2)}) copy-start(f32[3,6,197]{2,1,0:T(8,128)} %copy-done.29) | copy-start | bytes 42556
  329.6 7.2 %copy-start.38 = (f32[3,6,197]{2,1,0:T(8,128)S(1)}, f32[3,6,197]{2,1,0:T(8,128)}, u32[]{:S(2)}) copy-start(f32[3,6,197]{2,1,0:T(8,128)} %copy-done.37) | copy-start | bytes 42556
  329.6 7.2 %copy-start.15 = (f32[591,384]{1,0:T(8,128)S(1)}, f32[591,384]{1,0:T(8,128)}, u32[]{:S(2)}) copy-start(f32[591,384]{1,0:T(8,128)} %copy-done.14) | copy-start | bytes 2723332
  332.2 13.8 %copy-start.28 = (f32[591,8]{0,1:T(8,128)S(1)}, f32[591,8]{0,1:T(8,128)}, u32[]{:S(2)}) copy-start(f32[591,8]{0,1:T(8,128)} %copy-done.27) | copy-start | bytes 56740
  332.2 13.9 %copy-start.36 = (f32[591]{0:T(1024)S(1)}, f32[591]{0:T(1024)}, u32[]{:S(2)}) copy-start(f32[591]{0:T(1024)} %copy-done.35) | copy-start | bytes 7096
  332.2 22.0 %all-to-all-start.3 = ((bf16[4,2,236,384]{3,1,2,0:T(2,128)(2,1)}), bf16[4,2,236,384]{3,1,2,0:T(2,128)(2,1)}, u32[]{:S(2)}, u32[]{:S(2)}) async-start(bf16[4,2,236,384]{3,1,2,0:T(2,128)(2,1)} %copy.137), calls=%async_computation.3 | async-start | bytes 2899968 | tf_op jit(solution)/shard_map/all_to_all | solution.py:152
  336.7 92.7 %reduce-scatter.8.cloned.1.call-start = ((), (), s32[]{:S(2)}) async-start(), calls=%async_computation.9 | async-start | bytes 995328 | tf_op jit(solution)/shard_map/reduce_scatter | solution.py:207
  366.6 8.0 %copy-start.51 = (bf16[384,8]{0,1:T(8,128)(2,1)S(1)}, bf16[384,8]{0,1:T(8,128)(2,1)}, u32[]{:S(2)}) copy-start(bf16[384,8]{0,1:T(8,128)(2,1)} %copy-done.50) | copy-start | bytes 18436
  369.9 9.4 %copy-start.5 = (f32[3,197,384]{2,1,0:T(8,128)S(1)}, f32[3,197,384]{2,1,0:T(8,128)}, u32[]{:S(2)}) copy-start(f32[3,197,384]{2,1,0:T(8,128)} %copy-done.3) | copy-start | bytes 2723332
  369.9 9.4 %copy-start.34 = (f32[3,197]{1,0:T(4,128)S(1)}, f32[3,197]{1,0:T(4,128)}, u32[]{:S(2)}) copy-start(f32[3,197]{1,0:T(4,128)} %copy-done.33) | copy-start | bytes 7096
  369.9 9.4 %copy-start.53 = (f32[384]{0:T(512)S(1)}, f32[384]{0:T(512)}, u32[]{:S(2)}) copy-start(f32[384]{0:T(512)} %copy-done.52) | copy-start | bytes 4612
  369.9 11.1 %copy-start.60 = (f32[3,197]{1,0:T(4,128)S(1)}, f32[3,197]{1,0:T(4,128)}, u32[]{:S(2)}) copy-start(f32[3,197]{1,0:T(4,128)} %copy-done.59) | copy-start | bytes 7096
  369.9 11.1 %copy-start.49 = (f32[3,197]{1,0:T(4,128)S(1)}, f32[3,197]{1,0:T(4,128)}, u32[]{:S(2)}) copy-start(f32[3,197]{1,0:T(4,128)} %copy-done.48) | copy-start | bytes 7096
  398.1 62.9 %reduce-scatter.16.cloned.1.call-start = ((), (), s32[]{:S(2)}) async-start(), calls=%async_computation.14 | async-start | bytes 110592
  400.2 121.7 %reduce-scatter.10.cloned.1.call-start = ((), (), s32[]{:S(2)}) async-start(), calls=%async_computation.11 | async-start | bytes 331776 | tf_op jit(solution)/shard_map/reduce_scatter | solution.py:210
  402.5 138.7 %all-reduce.12.cloned.1.call-start = ((), (), s32[]{:S(2)}) async-start(), calls=%async_computation.10 | async-start | bytes 221184 | tf_op jit(solution)/shard_map/psum | solution.py:233
  429.4 146.1 %reduce-scatter.14.cloned.1.call-start = ((), (), s32[]{:S(2)}) async-start(), calls=%async_computation.13 | async-start | bytes 2654208 | tf_op jit(solution)/shard_map/reduce_scatter | solution.py:225
  437.8 175.9 %reduce-scatter.12.cloned.1.call-start = ((), (), s32[]{:S(2)}) async-start(), calls=%async_computation.12 | async-start | bytes 2654208 | tf_op jit(solution)/shard_map/reduce_scatter | solution.py:222
  445.1 57.9 %copy-start.58 = (f32[3,197]{1,0:T(4,128)S(1)}, f32[3,197]{1,0:T(4,128)}, u32[]{:S(2)}) copy-start(f32[3,197]{1,0:T(4,128)} %copy-done.57) | copy-start | bytes 7096
  (35 other events, 76.1 us)
Sparse Core Ops, SparseCore 0:
  398.2 31.0 reduce-scatter.7
  432.2 28.7 reduce-scatter.15
  463.8 29.2 reduce-scatter.9
  495.9 39.5 all-reduce.11
  537.7 37.7 reduce-scatter.13
  577.7 35.9 reduce-scatter.11
where the time goes:
time: 634 us; the launch traced here: 624 us
  blocking collectives  171 us (27%)
  waiting for transfers between devices  151 us (24%)
  local copies, waits for them, and re-layouts  114 us (18%)
  matrix products  90 us (14%)
  other arithmetic  60.2 us (9%)
  between operations  20.3 us (3%)
  starting transfers between devices  18.4 us (3%)
    psum x2, blocking collectives, body(): count, sq_total = lax.psum((local_count, local_sq), ('dp', 'expert'))  77.5 us
    reduce_scatter x1, waiting for transfers between devices, body(): lax.psum_scatter(d_in_part.astype(jnp.bfloat16), 'dp', scatter_dimension=...  36.4 us
    unnamed x2, blocking collectives  32.7 us
    reduce_scatter x1, waiting for transfers between devices, body(): lax.psum_scatter(d_back_part.astype(jnp.bfloat16), 'dp', scatter_dimensio...  32.7 us
    dot_general x1, matrix products, body(): jnp.einsum('secd,edf->secf', arrived, w_in, preferred_element_type=jnp.fl...  30.4 us
    reduce_scatter x1, waiting for transfers between devices, body(): lax.psum_scatter(d_qkv_part.astype(jnp.bfloat16), 'dp', scatter_dimension...  26.8 us
    gather x4, local copies, waits for them, and re-layouts, take_rows(): return jnp.take(padded, index, axis=0)  18.1 us
    psum x1, blocking collectives, body(): lax.psum(dense[1].astype(jnp.bfloat16), 'expert').astype(jnp.float32)  17 us
  transfers between devices with their start and end apart: 10, of which 7 were waited for; matrix products, arithmetic and copies ran while one was open for 10% of the time, Pallas kernels for 0%

commit v1 on v0

v1 whole, which is shorter than its diff:
```python
import functools
import math

import jax
import jax.numpy as jnp
from jax import lax
from jax.experimental import pallas as pl
from jax.experimental.pallas import tpu as pltpu
from jax.sharding import PartitionSpec as P

HEAD_DIM = 64
CORES = 2
LANES = 128
MESH = pl.DeviceIdType.MESH
F32 = jnp.float32
BF16 = jnp.bfloat16
ANY = pl.BlockSpec(memory_space=pl.ANY)
VMEM = pl.BlockSpec(memory_space=pltpu.VMEM)


def mm(a, b):
    return lax.dot_general(a, b, (((1,), (0,)), ((), ())), preferred_element_type=F32)


def mm_nt(a, b):
    return lax.dot_general(a, b, (((1,), (1,)), ((), ())), preferred_element_type=F32)


def mm_tn(a, b):
    return lax.dot_general(a, b, (((0,), (0,)), ((), ())), preferred_element_type=F32)


def iota(shape, dim):
    return lax.broadcasted_iota(jnp.int32, shape, dim)


def norm_stats(v):
    middle = jnp.mean(v, axis=-1, keepdims=True)
    center = v - middle
    variance = jnp.mean(center * center, axis=-1, keepdims=True)
    rstd = lax.rsqrt(variance + 1e-06)
    return center * rstd, rstd


def norm_back(grad, xhat, rstd, gain):
    inner = grad * gain
    first = jnp.mean(inner, axis=-1, keepdims=True)
    second = jnp.mean(inner * xhat, axis=-1, keepdims=True)
    return rstd * (inner - first - xhat * second)


def position():
    dp = lax.axis_index("dp")
    return dp // CORES, lax.rem(dp, CORES), lax.axis_index("expert")


def device(z, c, g):
    return {"dp": z * CORES + c, "expert": g}


def remote(src, dst, send_sem, recv_sem, where):
    return pltpu.make_async_remote_copy(
        src_ref=src,
        dst_ref=dst,
        send_sem=send_sem,
        recv_sem=recv_sem,
        device_id=where,
        device_id_type=MESH,
    )


def meet(peers):
    barrier = pltpu.get_barrier_semaphore()
    for peer in peers:
        pl.semaphore_signal(barrier, inc=1, device_id=peer, device_id_type=MESH)
    pl.semaphore_wait(barrier, len(peers))


def gather_kernel(n_z, shard, full, stage, send_z, recv_z, send_c, recv_c, local):
    z, c, g = position()
    own = z * CORES + c
    keep_in = pltpu.make_async_copy(shard, stage, local.at[0])
    keep_in.start()
    meet(
        [device(lax.rem(z + k, n_z), c, g) for k in range(1, n_z)]
        + [device(lax.rem(z + k, n_z), 1 - c, g) for k in range(n_z)]
    )

    def cross(src, index, slot):
        return remote(src, full.at[index], send_c.at[slot], recv_c.at[slot], device(z, 1 - c, g))

    cross(shard, own, 0).start()
    keep_in.wait()
    keep = pltpu.make_async_copy(stage, full.at[own], local.at[1])
    keep.start()
    for k in range(n_z - 1):
        for way in range(2):
            step = 1 - 2 * way
            origin = z - step * k
            index = lax.rem(origin + n_z, n_z) * CORES + c
            to = lax.rem(z + step + n_z, n_z)
            inside = (origin >= 0) & (origin < n_z) & (z + step >= 0) & (z + step < n_z)

            @pl.when(inside)
            def _():
                src = shard if k == 0 else full.at[index]
                remote(
                    src, full.at[index], send_z.at[way, k], recv_z.at[way, k], device(to, c, g)
                ).start()

        for way in range(2):
            step = 1 - 2 * way
            origin = z - step * (k + 1)
            index = lax.rem(origin + n_z, n_z) * CORES + c

            @pl.when((origin >= 0) & (origin < n_z))
            def _():
                remote(
                    shard, full.at[index], send_z.at[way, k], recv_z.at[way, k], device(z, 1 - c, g)
                ).wait_recv()
                cross(full.at[index], index, 1 + 2 * k + way).start()

    for k in range(n_z - 1):
        for way in range(2):
            step = 1 - 2 * way
            origin = z - step * k
            inside = (origin >= 0) & (origin < n_z) & (z + step >= 0) & (z + step < n_z)

            @pl.when(inside)
            def _():
                remote(
                    shard, full.at[own], send_z.at[way, k], recv_z.at[way, k], device(z, 1 - c, g)
                ).wait_send()

            origin = z - step * (k + 1)

            @pl.when((origin >= 0) & (origin < n_z))
            def _():
                cross(shard, own, 1 + 2 * k + way).wait()

    cross(shard, own, 0).wait()
    keep.wait()


def gather_weights(shard, n_dp):
    n_z = n_dp // CORES
    rows, cols = shard.shape
    return pl.pallas_call(
        functools.partial(gather_kernel, n_z),
        out_shape=jax.ShapeDtypeStruct((n_dp, rows, cols), shard.dtype),
        in_specs=[ANY],
        out_specs=ANY,
        scratch_shapes=[
            pltpu.VMEM((rows, cols), shard.dtype),
            pltpu.SemaphoreType.DMA((2, n_z - 1)),
            pltpu.SemaphoreType.DMA((2, n_z - 1)),
            pltpu.SemaphoreType.DMA((2 * n_z - 1,)),
            pltpu.SemaphoreType.DMA((2 * n_z - 1,)),
            pltpu.SemaphoreType.DMA((2,)),
        ],
        compiler_params=pltpu.CompilerParams(
            collective_id=0, has_side_effects=True, vmem_limit_bytes=4 << 20
        ),
        name="gather_weights",
    )(shard).reshape(n_dp * rows, cols)


def swap_kernel(parts, n_z, plane, sent, tile, arrived, tiles, stage, small, sends, recvs, tsend, trecv, local):
    z, c, g = position()
    me = g * CORES + c
    keep_in = pltpu.make_async_copy(sent.at[me], stage, local.at[0])
    keep_in.start()
    tile_in = pltpu.make_async_copy(tile, small, local.at[1])
    tile_in.start()
    others = [lax.rem(me + k, parts) for k in range(1, parts)]
    plane_peers = [device(z, lax.rem(e, CORES), e // CORES) for e in others]
    z_peers = [device(lax.rem(z + k, n_z), c, g) for k in range(1, n_z)]
    tile_peers = plane_peers if plane else z_peers
    tile_me = me if plane else z
    meet(plane_peers if plane else plane_peers + z_peers)
    copies = [
        remote(sent.at[e], arrived.at[me], sends.at[k], recvs.at[k], where)
        for k, (e, where) in enumerate(zip(others, plane_peers))
    ]
    copies += [
        remote(tile, tiles.at[tile_me], tsend.at[k], trecv.at[k], where)
        for k, where in enumerate(tile_peers)
    ]
    for copy in copies:
        copy.start()
    keep_in.wait()
    keep = pltpu.make_async_copy(stage, arrived.at[me], local.at[0])
    keep.start()
    tile_in.wait()
    tile_keep = pltpu.make_async_copy(small, tiles.at[tile_me], local.at[1])
    tile_keep.start()
    for copy in copies:
        copy.wait()
    keep.wait()
    tile_keep.wait()


def swap(sent, tile, n_z, plane, number):
    parts = sent.shape[0]
    count = parts if plane else n_z
    return pl.pallas_call(
        functools.partial(swap_kernel, parts, n_z, plane),
        out_shape=(
            jax.ShapeDtypeStruct(sent.shape, sent.dtype),
            jax.ShapeDtypeStruct((count, *tile.shape), tile.dtype),
        ),
        in_specs=[ANY, ANY],
        out_specs=(ANY, ANY),
        scratch_shapes=[
            pltpu.VMEM(sent.shape[1:], sent.dtype),
            pltpu.VMEM(tile.shape, tile.dtype),
            pltpu.SemaphoreType.DMA((parts - 1,)),
            pltpu.SemaphoreType.DMA((parts - 1,)),
            pltpu.SemaphoreType.DMA((count - 1,)),
            pltpu.SemaphoreType.DMA((count - 1,)),
            pltpu.SemaphoreType.DMA((2,)),
        ],
        compiler_params=pltpu.CompilerParams(
            collective_id=number, has_side_effects=True, vmem_limit_bytes=4 << 20
        ),
        name=f"swap_{number}",
    )(sent, tile)


def front_kernel(
    experts, slots, image, routes, routes_t, weights,
    proj_out, probs_out, mixed_out, hidden_out, meta_out, meta_t_out, sent_out, carry, carry_t,
):
    step = pl.program_id(0)
    width = image.shape[-1]
    seq = image.shape[1]
    heads = width // HEAD_DIM

    @pl.when(step == 0)
    def _():
        carry[...] = jnp.zeros_like(carry)
        carry_t[...] = jnp.zeros_like(carry_t)

    w_qkv = weights[:, : 3 * width]
    w_out = weights[:, 3 * width : 4 * width]
    misc = weights[:, 4 * width :]
    misc_t = misc.astype(F32).T
    gain_one = misc_t[experts : experts + 1]
    gain_two = misc_t[experts + 1 : experts + 2]
    x = image[0].astype(F32)
    xhat, _ = norm_stats(x)
    normed = (xhat * gain_one).astype(BF16)
    proj_out[0] = mm(normed, w_qkv).astype(BF16)
    scale = HEAD_DIM ** (-0.5)
    lower = iota((seq, LANES), 1) < HEAD_DIM
    for pair in range(heads // 2):
        at = pair * LANES
        query = proj_out[0, :, at : at + LANES]
        keys = proj_out[0, :, width + at : width + at + LANES]
        values = proj_out[0, :, 2 * width + at : 2 * width + at + LANES]
        outs = []
        for half in range(2):
            mask = lower if half == 0 else jnp.logical_not(lower)
            part = jnp.where(mask, query, jnp.zeros_like(query))
            scores = mm_nt(part, keys) * scale
            shifted = jnp.exp(scores - jnp.max(scores, axis=-1, keepdims=True))
            probs = shifted / jnp.sum(shifted, axis=-1, keepdims=True)
            probs_out[0, 2 * pair + half] = probs
            outs.append(mm(probs.astype(BF16), values))
        mixed_out[0, :, at : at + LANES] = jnp.where(lower, outs[0], outs[1]).astype(BF16)
    hidden = x + mm(mixed_out[0], w_out)
    hidden_out[0] = hidden
    hhat, _ = norm_stats(hidden)
    normed_two = (hhat * gain_two).astype(BF16)
    logits = mm(normed_two, misc)

    lane = iota((seq, LANES), 1)
    hit = [lane == routes[0, :, k : k + 1] for k in range(2)]
    own = [jnp.sum(jnp.where(h, logits, 0.0), axis=1, keepdims=True) for h in hit]
    gates = [1.0 / (1.0 + jnp.exp(own[1 - k] - own[k])) for k in range(2)]
    hits = jnp.where(hit[0] | hit[1], 1.0, 0.0)
    before = jnp.where(iota((seq, seq), 1) < iota((seq, seq), 0), 1.0, 0.0).astype(BF16)
    order = mm(before, hits.astype(BF16)) + carry[...]
    carry[...] += jnp.sum(hits, axis=0, keepdims=True)
    place = [
        routes[0, :, k : k + 1].astype(F32) * slots
        + jnp.sum(jnp.where(hit[k], order, 0.0), axis=1, keepdims=True)
        for k in range(2)
    ]
    meta = jnp.where(lane == 0, gates[0], jnp.where(lane == 1, gates[1], 0.0))
    meta_out[0] = jnp.where(lane == 2, place[0], jnp.where(lane == 3, place[1], meta))

    depth = carry_t.shape[0]
    row = iota((depth, seq), 0)
    hit_t = [row == routes_t[0, k : k + 1, :] for k in range(2)]
    hits_t = jnp.where(hit_t[0] | hit_t[1], 1.0, 0.0)
    after = jnp.where(iota((seq, seq), 0) < iota((seq, seq), 1), 1.0, 0.0).astype(BF16)
    order_t = mm(hits_t.astype(BF16), after) + carry_t[...]
    carry_t[...] += jnp.sum(hits_t, axis=1, keepdims=True)
    place_t = [
        routes_t[0, k : k + 1, :].astype(F32) * slots
        + jnp.sum(jnp.where(hit_t[k], order_t, 0.0), axis=0, keepdims=True)
        for k in range(2)
    ]
    for k in range(2):
        meta_t_out[0, k : k + 1, :] = place_t[k]

    def send(e, _):
        at = (iota((slots, seq), 0) + e * slots).astype(F32)
        pick = jnp.where((at == place_t[0]) | (at == place_t[1]), 1.0, 0.0).astype(BF16)
        rows = mm(pick, normed_two).astype(BF16)

        @pl.when(step == 0)
        def _():
            sent_out[e] = rows

        @pl.when(step > 0)
        def _():
            sent_out[e] = sent_out[e] + rows

        return 0

    lax.fori_loop(0, experts, send, 0)


def front(images, routes, weights, experts, slots):
    count, seq, width = images.shape
    heads = width // HEAD_DIM
    depth = -(-experts // 16) * 16
    routes_t = jnp.swapaxes(routes, 1, 2)

    def per_image(*shape):
        return pl.BlockSpec((1, *shape), lambda i: (i,) + (0,) * len(shape))

    def whole(*shape):
        return pl.BlockSpec(shape, lambda i: (0,) * len(shape))

    return pl.pallas_call(
        functools.partial(front_kernel, experts, slots),
        grid=(count,),
        out_shape=(
            jax.ShapeDtypeStruct((count, seq, 3 * width), BF16),
            jax.ShapeDtypeStruct((count, heads, seq, seq), F32),
            jax.ShapeDtypeStruct((count, seq, width), BF16),
            jax.ShapeDtypeStruct((count, seq, width), F32),
            jax.ShapeDtypeStruct((count, seq, LANES), F32),
            jax.ShapeDtypeStruct((count, 2, seq), F32),
            jax.ShapeDtypeStruct((experts, slots, width), BF16),
        ),
        in_specs=[
            per_image(seq, width),
            per_image(seq, 2),
            per_image(2, seq),
            whole(*weights.shape),
        ],
        out_specs=(
            per_image(seq, 3 * width),
            per_image(heads, seq, seq),
            per_image(seq, width),
            per_image(seq, width),
            per_image(seq, LANES),
            per_image(2, seq),
            whole(experts, slots, width),
        ),
        scratch_shapes=[pltpu.VMEM((1, LANES), F32), pltpu.VMEM((depth, 1), F32)],
        name="front",
    )(images, routes, routes_t, weights)


def gelu_pair(v):
    size = jnp.abs(v)
    t = 1.0 / (1.0 + (0.3275911 * math.sqrt(0.5)) * size)
    bell = jnp.exp(v * v * (-0.5))
    poly = t * (
        0.127414796
        + t * (-0.142248368 + t * (0.7107068705 + t * (-0.7265760135 + t * 0.5307027145)))
    )
    tail = poly * bell
    phi = jnp.where(v >= 0.0, 1.0 - tail, tail)
    return v * phi, phi + v * bell * (1.0 / math.sqrt(2.0 * math.pi))


def expert_kernel(core, x, w_in, w_back, tiles, act_out, slope_out, made_out, tile_out):
    hidden = w_in.shape[-1]
    block = 256
    rows = x[...]
    for n in range(hidden // block):
        cols = slice(n * block, (n + 1) * block)
        act, slope = gelu_pair(mm(rows, w_in[0, :, cols]))
        act_out[:, cols] = act.astype(BF16)
        slope_out[:, cols] = slope.astype(BF16)
    made_out[...] = mm(act_out[...], w_back[0]).astype(BF16)
    total = tiles[0]
    for k in range(1, tiles.shape[0]):
        total += tiles[k]
    tile_out[...] = total


def row_tile(rows):
    return rows // 4


def expert_forward(core, x, w_in, w_back, tiles):
    rows, width = x.shape
    hidden = w_in.shape[-1]
    tile = row_tile(rows)
    row_block = lambda cols: pl.BlockSpec((tile, cols), lambda i, c: (i, 0))
    return pl.pallas_call(
        expert_kernel,
        grid_spec=pltpu.PrefetchScalarGridSpec(
            num_scalar_prefetch=1,
            grid=(rows // tile,),
            in_specs=[
                row_block(width),
                pl.BlockSpec((1, width, hidden), lambda i, c: (c[0], 0, 0)),
                pl.BlockSpec((1, hidden, width), lambda i, c: (c[0], 0, 0)),
                pl.BlockSpec(tiles.shape, lambda i, c: (0, 0, 0)),
            ],
            out_specs=[
                row_block(hidden),
                row_block(hidden),
                row_block(width),
                pl.BlockSpec(tiles.shape[1:], lambda i, c: (0, 0)),
            ],
        ),
        out_shape=(
            jax.ShapeDtypeStruct((rows, hidden), BF16),
            jax.ShapeDtypeStruct((rows, hidden), BF16),
            jax.ShapeDtypeStruct((rows, width), BF16),
            jax.ShapeDtypeStruct(tiles.shape[1:], F32),
        ),
        name="expert_forward",
    )(core, x, w_in, w_back, tiles)


def middle_kernel(
    total_rows, experts, slots, back, hidden, meta, meta_t, teacher, out_grad, valid, tiles,
    output, grad_out, grad_logits, sent_out, square_out, count_out, squares, routes,
):
    step = pl.program_id(0)
    seq, width = hidden.shape[1:]
    count = jnp.sum(tiles[...], axis=0)[0:1, 0:1]
    places = [meta[0, :, 2 + k : 3 + k] for k in range(2)]
    gates = [meta[0, :, k : k + 1] for k in range(2)]
    all_slots = experts * slots
    chunk = chunk_of(all_slots)
    picked = [jnp.zeros((seq, width), F32) for _ in range(2)]
    for n in range(all_slots // chunk):
        at = (iota((seq, chunk), 1) + n * chunk).astype(F32)
        rows = back[n * chunk : (n + 1) * chunk]
        for k in range(2):
            pick = jnp.where(at == places[k], 1.0, 0.0).astype(BF16)
            picked[k] += mm(pick, rows)
    combined = hidden[0] + (gates[0] * picked[0] + gates[1] * picked[1])
    output[0] = combined.astype(BF16)
    diff = combined - teacher[0].astype(F32)
    masked = valid[0] * diff
    sq = jnp.sum(jnp.sum(masked * diff, axis=1, keepdims=True), axis=0, keepdims=True)

    @pl.when(step == 0)
    def _():
        squares[...] = jnp.zeros_like(squares)

    squares[...] += sq
    square_out[...] = squares[...]
    count_out[...] = jnp.zeros_like(count_out) + count
    grad = out_grad[0].astype(F32) + (total_rows / count) * masked
    grad_out[0] = grad
    grad_gates = [jnp.sum(p * grad, axis=1, keepdims=True) for p in picked]
    slope = gates[0] * gates[1] * (grad_gates[0] - grad_gates[1])
    lane = iota((seq, LANES), 1)
    hit = [lane == routes[0, :, k : k + 1] for k in range(2)]
    grad_logits[0] = jnp.where(hit[0], slope, jnp.where(hit[1], -slope, 0.0)).astype(BF16)
    weighted = [(g * grad).astype(BF16) for g in gates]
    places_t = [meta_t[0, k : k + 1, :] for k in range(2)]

    def send(e, _):
        at = (iota((slots, seq), 0) + e * slots).astype(F32)
        rows = jnp.zeros((slots, width), F32)
        for k in range(2):
            pick = jnp.where(at == places_t[k], 1.0, 0.0).astype(BF16)
            rows += mm(pick, weighted[k])
        rows = rows.astype(BF16)

        @pl.when(step == 0)
        def _():
            sent_out[e] = rows

        @pl.when(step > 0)
        def _():
            sent_out[e] = sent_out[e] + rows

        return 0

    lax.fori_loop(0, experts, send, 0)


def chunk_of(total):
    for chunk in (640, 512, 384, 256, 128):
        if total % chunk == 0:
            return chunk
    return total


def middle(total_rows, back, hidden, meta, meta_t, teacher, out_grad, valid, tiles, routes, experts, slots):
    count, seq, width = hidden.shape

    def per_image(*shape):
        return pl.BlockSpec((1, *shape), lambda i: (i,) + (0,) * len(shape))

    def whole(*shape):
        return pl.BlockSpec(shape, lambda i: (0,) * len(shape))

    def body(*refs):
        ins, route, rest = refs[:8], refs[8], refs[9:]
        middle_kernel(total_rows, experts, slots, *ins, *rest, route)

    return pl.pallas_call(
        body,
        grid=(count,),
        out_shape=(
            jax.ShapeDtypeStruct((count, seq, width), BF16),
            jax.ShapeDtypeStruct((count, seq, width), F32),
            jax.ShapeDtypeStruct((count, seq, LANES), BF16),
            jax.ShapeDtypeStruct((experts, slots, width), BF16),
            jax.ShapeDtypeStruct((8, LANES), F32),
            jax.ShapeDtypeStruct((8, LANES), F32),
        ),
        in_specs=[
            whole(*back.shape),
            per_image(seq, width),
            per_image(seq, LANES),
            per_image(2, seq),
            per_image(seq, width),
            per_image(seq, width),
            per_image(seq, 1),
            whole(*tiles.shape),
            per_image(seq, 2),
        ],
        out_specs=(
            per_image(seq, width),
            per_image(seq, width),
            per_image(seq, LANES),
            whole(experts, slots, width),
            whole(8, LANES),
            whole(8, LANES),
        ),
        scratch_shapes=[pltpu.VMEM((8, LANES), F32)],
        name="middle",
    )(back, hidden, meta, meta_t, teacher, out_grad, valid, tiles, routes)


def expert_back_kernel(core, grad, x, act, slope, w_in, w_back, grad_x, d_in, d_back, pre, sum_in, sum_back):
    step = pl.program_id(0)
    hidden = w_in.shape[-1]
    block = 256

    @pl.when(step == 0)
    def _():
        sum_in[...] = jnp.zeros_like(sum_in)
        sum_back[...] = jnp.zeros_like(sum_back)

    rows = grad[...]
    rows_t = rows.T
    x_t = x[...].T
    for n in range(hidden // block):
        cols = slice(n * block, (n + 1) * block)
        pre[:, cols] = (mm_nt(rows, w_back[0, cols, :]) * slope[:, cols].astype(F32)).astype(BF16)
        sum_back[:, cols] += mm(rows_t, act[:, cols])
        sum_in[:, cols] += mm(x_t, pre[:, cols])
    grad_x[...] = mm_nt(pre[...], w_in[0]).astype(BF16)

    @pl.when(step == pl.num_programs(0) - 1)
    def _():
        d_in[...] = sum_in[...].astype(BF16)
        for n in range(hidden // block):
            cols = slice(n * block, (n + 1) * block)
            d_back[cols, :] = sum_back[:, cols].T.astype(BF16)


def expert_backward(core, grad, x, act, slope, w_in, w_back):
    rows, width = x.shape
    hidden = w_in.shape[-1]
    tile = row_tile(rows)
    row_block = lambda cols: pl.BlockSpec((tile, cols), lambda i, c: (i, 0))
    return pl.pallas_call(
        expert_back_kernel,
        grid_spec=pltpu.PrefetchScalarGridSpec(
            num_scalar_prefetch=1,
            grid=(rows // tile,),
            in_specs=[
                row_block(width),
                row_block(width),
                row_block(hidden),
                row_block(hidden),
                pl.BlockSpec((1, width, hidden), lambda i, c: (c[0], 0, 0)),
                pl.BlockSpec((1, hidden, width), lambda i, c: (c[0], 0, 0)),
            ],
            out_specs=[
                row_block(width),
                pl.BlockSpec((width, hidden), lambda i, c: (0, 0)),
                pl.BlockSpec((hidden, width), lambda i, c: (0, 0)),
            ],
            scratch_shapes=[
                pltpu.VMEM((tile, hidden), BF16),
                pltpu.VMEM((width, hidden), F32),
                pltpu.VMEM((width, hidden), F32),
            ],
        ),
        out_shape=(
            jax.ShapeDtypeStruct((rows, width), BF16),
            jax.ShapeDtypeStruct((width, hidden), BF16),
            jax.ShapeDtypeStruct((hidden, width), BF16),
        ),
        name="expert_backward",
    )(core, grad, x, act, slope, w_in, w_back)


def piece_shape(n_g, rows, cols):
    row_parts = 2 if rows % 16 == 0 and n_g % 2 == 0 else 1
    col_parts = n_g // row_parts
    tiles = -(-cols // (LANES * col_parts))
    return row_parts, col_parts, rows // row_parts, tiles * LANES


def rear_kernel(
    experts, pieces, home, image, hidden, grad_out, grad_logits, meta, proj, probs, mixed, weights,
    grad_image, dense, sum_qkv, sum_out, sum_misc, grad_proj,
):
    step = pl.program_id(0)
    seq, width = image.shape[1:]
    heads = width // HEAD_DIM

    @pl.when(step == 0)
    def _():
        sum_qkv[...] = jnp.zeros_like(sum_qkv)
        sum_out[...] = jnp.zeros_like(sum_out)
        sum_misc[...] = jnp.zeros_like(sum_misc)

    w_qkv = weights[:, : 3 * width]
    w_out = weights[:, 3 * width : 4 * width]
    misc_t = weights[:, 4 * width :].astype(F32).T
    gain_one = misc_t[experts : experts + 1]
    gain_two = misc_t[experts + 1 : experts + 2]
    places = [meta[0, :, 2 + k : 3 + k] for k in range(2)]
    all_slots = home.shape[0]
    chunk = chunk_of(all_slots)
    logit_rows = grad_logits[0]
    grad_two = mm(logit_rows, misc_t.astype(BF16))
    for n in range(all_slots // chunk):
        at = (iota((seq, chunk), 1) + n * chunk).astype(F32)
        pick = jnp.where((at == places[0]) | (at == places[1]), 1.0, 0.0).astype(BF16)
        grad_two += mm(pick, home[n * chunk : (n + 1) * chunk])
    hhat, h_rstd = norm_stats(hidden[0])
    normed_two = (hhat * gain_two).astype(BF16)
    d_gain_two = jnp.sum(grad_two * hhat, axis=0, keepdims=True)
    grad_hidden = grad_out[0] + norm_back(grad_two, hhat, h_rstd, gain_two)
    grad_attn = grad_hidden.astype(BF16)
    sum_out[...] += mm_tn(mixed[0], grad_attn)
    grad_mixed = mm_nt(grad_attn, w_out).astype(BF16)
    d_router = mm_tn(logit_rows, normed_two)

    scale = HEAD_DIM ** (-0.5)
    lower = iota((seq, LANES), 1) < HEAD_DIM
    for pair in range(heads // 2):
        at = pair * LANES
        query = proj[0, :, at : at + LANES]
        keys = proj[0, :, width + at : width + at + LANES]
        values = proj[0, :, 2 * width + at : 2 * width + at + LANES]
        grad_pair = grad_mixed[:, at : at + LANES]
        got = []
        for half in range(2):
            mask = lower if half == 0 else jnp.logical_not(lower)
            part = jnp.where(mask, grad_pair, jnp.zeros_like(grad_pair))
            prob = probs[0, 2 * pair + half]
            grad_probs = mm_nt(part, values)
            inner = jnp.sum(grad_probs * prob, axis=-1, keepdims=True)
            grad_scores = (prob * (grad_probs - inner)).astype(BF16)
            got.append(
                (
                    mm(grad_scores, keys) * scale,
                    mm_tn(grad_scores, query) * scale,
                    mm_tn(prob.astype(BF16), grad_pair),
                )
            )
        for which in range(3):
            start = which * width + at
            grad_proj[:, start : start + LANES] = jnp.where(lower, got[0][which], got[1][which]).astype(BF16)
    xhat, x_rstd = norm_stats(image[0].astype(F32))
    normed_one = (xhat * gain_one).astype(BF16)
    sum_qkv[...] += mm_tn(normed_one, grad_proj[...])
    grad_one = mm_nt(grad_proj[...], w_qkv)
    d_gain_one = jnp.sum(grad_one * xhat, axis=0, keepdims=True)
    grad_image[0] = (grad_hidden + norm_back(grad_one, xhat, x_rstd, gain_one)).astype(BF16)
    row = iota((LANES, width), 0)
    sum_misc[...] += jnp.where(
        row == experts, d_gain_one, jnp.where(row == experts + 1, d_gain_two, d_router)
    )

    @pl.when(step == pl.num_programs(0) - 1)
    def _():
        n_z, blk, (row_parts, col_parts, rows, cols) = pieces
        misc = sum_misc[...].T
        for z in range(n_z):
            for c in range(CORES):
                for r in range(row_parts):
                    top = (z * CORES + c) * blk + r * rows
                    for tile in range(col_parts * cols // LANES):
                        left = tile * LANES
                        q, inside = left // cols, left % cols
                        if left < 3 * width:
                            value = sum_qkv[top : top + rows, left : left + LANES]
                        elif left < 4 * width:
                            value = sum_out[top : top + rows, left - 3 * width : left - 3 * width + LANES]
                        elif left == 4 * width:
                            value = misc[top : top + rows]
                        else:
                            value = jnp.zeros((rows, LANES), F32)
                        dense[c, r * col_parts + q, z, :, inside : inside + LANES] = value.astype(BF16)


def rear(home, images, hidden, grad_out, grad_logits, meta, proj, probs, mixed, weights, experts, n_z, n_g):
    count, seq, width = images.shape
    blk = width // (n_z * CORES)
    parts = piece_shape(n_g, blk, 4 * width + LANES)

    def per_image(*shape):
        return pl.BlockSpec((1, *shape), lambda i: (i,) + (0,) * len(shape))

    def whole(*shape):
        return pl.BlockSpec(shape, lambda i: (0,) * len(shape))

    dense = (CORES, n_g, n_z, parts[2], parts[3])
    return pl.pallas_call(
        functools.partial(rear_kernel, experts, (n_z, blk, parts)),
        grid=(count,),
        out_shape=(
            jax.ShapeDtypeStruct((count, seq, width), BF16),
            jax.ShapeDtypeStruct(dense, BF16),
        ),
        in_specs=[
            whole(*home.shape),
            per_image(seq, width),
            per_image(seq, width),
            per_image(seq, width),
            per_image(seq, LANES),
            per_image(seq, LANES),
            per_image(seq, 3 * width),
            per_image(*probs.shape[1:]),
            per_image(seq, width),
            whole(*weights.shape),
        ],
        out_specs=(per_image(seq, width), whole(*dense)),
        scratch_shapes=[
            pltpu.VMEM((width, 3 * width), F32),
            pltpu.VMEM((width, width), F32),
            pltpu.VMEM((LANES, width), F32),
            pltpu.VMEM((seq, 3 * width), BF16),
        ],
        name="rear",
    )(home, images, hidden, grad_out, grad_logits, meta, proj, probs, mixed, weights)


def reduce_kernel(
    n_z, n_g, width, parts, d_in, d_back, dense, square, count,
    out_in, out_back, out_qkv, out_out, out_misc, out_loss,
    own_in, own_back, got_in, got_back, give_in, give_back, take_in, take_back,
    own_dense, got_dense, sum_dense, got_sum, own_piece, all_pieces, sq_plane, sq_give, sq_line,
    s_exp, r_exp, s_core, r_core, s_a, r_a, s_b, r_b, s_c, r_c, s_q, r_q, s_l, r_l, local,
):
    z, c, g = position()
    me = g * CORES + c
    members = n_g * CORES
    row_parts, col_parts, rows, cols = parts
    others = [lax.rem(me + k, members) for k in range(1, members)]
    plane = [device(z, lax.rem(e, CORES), e // CORES) for e in others]
    line_z = [lax.rem(z + k, n_z) for k in range(1, n_z)]
    line = [device(other, c, g) for other in line_z]
    loads = [
        pltpu.make_async_copy(d_in.at[z], own_in, local.at[0]),
        pltpu.make_async_copy(d_back.at[z], own_back, local.at[1]),
        pltpu.make_async_copy(dense.at[c, g], own_dense, local.at[2]),
    ]
    for load in loads:
        load.start()
    meet(plane + line)
    step_a = [
        remote(
            dense.at[lax.rem(e, CORES), e // CORES], got_dense.at[k], s_a.at[k], r_a.at[k], where
        )
        for k, (e, where) in enumerate(zip(others, plane))
    ]
    step_q = [
        remote(square, sq_plane.at[k], s_q.at[k], r_q.at[k], where) for k, where in enumerate(plane)
    ]
    heavy = []
    for k, (other, where) in enumerate(zip(line_z, line)):
        heavy.append(remote(d_in.at[other], got_in.at[k], s_exp.at[0, k], r_exp.at[0, k], where))
        heavy.append(remote(d_back.at[other], got_back.at[k], s_exp.at[1, k], r_exp.at[1, k], where))
    for copy in step_a + step_q + heavy:
        copy.start()
    for load in loads:
        load.wait()
    for copy in step_a + step_q:
        copy.wait()
    for k in range(n_z):
        total = own_dense[k].astype(F32)
        for m in range(members - 1):
            total += got_dense[m, k].astype(F32)
        sum_dense[k] = total.astype(BF16)
    total = square[...]
    for m in range(members - 1):
        total += sq_plane[m]
    sq_give[...] = total
    step_b = [
        remote(sum_dense.at[other], got_sum.at[k], s_b.at[k], r_b.at[k], where)
        for k, (other, where) in enumerate(zip(line_z, line))
    ]
    step_l = [
        remote(sq_give, sq_line.at[k], s_l.at[k], r_l.at[k], where) for k, where in enumerate(line)
    ]
    for copy in step_b + step_l:
        copy.start()
    for copy in step_b + step_l:
        copy.wait()
    total = sum_dense[z].astype(F32)
    for k in range(n_z - 1):
        total += got_sum[k].astype(F32)
    own_piece[...] = total.astype(BF16)
    all_pieces[g] = own_piece[...]
    step_c = [
        remote(
            own_piece, all_pieces.at[g], s_c.at[k], r_c.at[k], device(z, c, lax.rem(g + k + 1, n_g))
        )
        for k in range(n_g - 1)
    ]
    for copy in step_c:
        copy.start()
    total = sq_give[...]
    for k in range(n_z - 1):
        total += sq_line[k]
    out_loss[...] = total / (count[...] * width)
    for copy in step_c:
        copy.wait()
    for r in range(row_parts):
        for tile in range(4 * width // LANES + 1):
            left = tile * LANES
            q, inside = left // cols, left % cols
            value = all_pieces[r * col_parts + q, :, inside : inside + LANES].astype(F32)
            span = slice(r * rows, (r + 1) * rows)
            if left < 3 * width:
                out_qkv[span, left : left + LANES] = value
            elif left < 4 * width:
                out_out[span, left - 3 * width : left - 3 * width + LANES] = value
            else:
                out_misc[span, :] = value

    for copy in heavy:
        copy.wait()
    for own, got, give, out in ((own_in, got_in, give_in, out_in), (own_back, got_back, give_back, out_back)):

        def total_of(half):
            total = own[half].astype(F32)
            for k in range(n_z - 1):
                total += got[k, half].astype(F32)
            return total

        give[...] = total_of(1 - c).astype(BF16)
        out[c] = total_of(c)
    partner = device(z, 1 - c, g)
    last = [
        remote(give_in, take_in, s_core.at[0], r_core.at[0], partner),
        remote(give_back, take_back, s_core.at[1], r_core.at[1], partner),
    ]
    for copy in last:
        copy.start()
    for copy in last:
        copy.wait()
    out_in[1 - c] = take_in[...].astype(F32)
    out_back[1 - c] = take_back[...].astype(F32)


def reduce_all(d_in, d_back, dense, square, count, n_z, n_g):
    width, hidden = d_in.shape
    blk_in = width // (n_z * CORES)
    blk_back = hidden // (n_z * CORES)
    parts = piece_shape(n_g, blk_in, 4 * width + LANES)
    members = n_g * CORES
    piece = dense.shape[-2:]
    dma = pltpu.SemaphoreType.DMA
    return pl.pallas_call(
        functools.partial(reduce_kernel, n_z, n_g, width, parts),
        out_shape=(
            jax.ShapeDtypeStruct((CORES, blk_in, hidden), F32),
            jax.ShapeDtypeStruct((CORES, blk_back, width), F32),
            jax.ShapeDtypeStruct((blk_in, 3 * width), F32),
            jax.ShapeDtypeStruct((blk_in, width), F32),
            jax.ShapeDtypeStruct((blk_in, LANES), F32),
            jax.ShapeDtypeStruct((8, LANES), F32),
        ),
        in_specs=[ANY, ANY, ANY, VMEM, VMEM],
        out_specs=(VMEM,) * 6,
        scratch_shapes=[
            pltpu.VMEM((CORES, blk_in, hidden), BF16),
            pltpu.VMEM((CORES, blk_back, width), BF16),
            pltpu.VMEM((n_z - 1, CORES, blk_in, hidden), BF16),
            pltpu.VMEM((n_z - 1, CORES, blk_back, width), BF16),
            pltpu.VMEM((blk_in, hidden), BF16),
            pltpu.VMEM((blk_back, width), BF16),
            pltpu.VMEM((blk_in, hidden), BF16),
            pltpu.VMEM((blk_back, width), BF16),
            pltpu.VMEM((n_z, *piece), BF16),
            pltpu.VMEM((members - 1, n_z, *piece), BF16),
            pltpu.VMEM((n_z, *piece), BF16),
            pltpu.VMEM((n_z - 1, *piece), BF16),
            pltpu.VMEM(piece, BF16),
            pltpu.VMEM((n_g, *piece), BF16),
            pltpu.VMEM((members - 1, 8, LANES), F32),
            pltpu.VMEM((8, LANES), F32),
            pltpu.VMEM((n_z - 1, 8, LANES), F32),
            dma((2, n_z - 1)),
            dma((2, n_z - 1)),
            dma((2,)),
            dma((2,)),
            dma((members - 1,)),
            dma((members - 1,)),
            dma((n_z - 1,)),
            dma((n_z - 1,)),
            dma((n_g - 1,)),
            dma((n_g - 1,)),
            dma((members - 1,)),
            dma((members - 1,)),
            dma((n_z - 1,)),
            dma((n_z - 1,)),
            dma((3,)),
        ],
        compiler_params=pltpu.CompilerParams(
            collective_id=5, has_side_effects=True, vmem_limit_bytes=32 << 20
        ),
        name="reduce_all",
    )(
        d_in.reshape(n_z, CORES, blk_in, hidden),
        d_back.reshape(n_z, CORES, blk_back, width),
        dense,
        square,
        count,
    )


def body(
    images, teacher, out_grad, valid_mask, routes, w_qkv, w_out, gain_attn, gain_moe, router, w_in, w_back
):
    img_count, seq, width = images.shape
    n_dp, n_g = lax.axis_size("dp"), lax.axis_size("expert")
    n_z = n_dp // CORES
    experts = n_g * w_in.shape[0]
    rows = img_count * seq
    capacity = max(2, rows * 16 // (experts * 5))
    slots = -(-capacity // 16) * 16
    total_rows = rows * n_dp * n_g
    core = lax.rem(lax.axis_index("dp"), CORES).astype(jnp.int32).reshape(1)
    valid = valid_mask.astype(F32)
    tile = jnp.zeros((8, LANES), F32) + jnp.sum(valid)
    shard = jnp.concatenate(
        [
            w_qkv,
            w_out,
            router,
            gain_attn[:, None],
            gain_moe[:, None],
            jnp.zeros((router.shape[0], LANES - experts - 2), BF16),
        ],
        axis=1,
    )
    weights = gather_weights(shard, n_dp)
    proj, probs, mixed, hidden, meta, meta_t, sent = front(images, routes, weights, experts, slots)
    arrived, tiles = swap(sent, tile, n_z, True, 1)
    x = arrived.reshape(experts * slots, width)
    act, slope, made, tile = expert_forward(core, x, w_in, w_back, tiles)
    back, tiles = swap(made.reshape(experts, slots, width), tile, n_z, False, 2)
    output, grad_out, grad_logits, sent, square, count = middle(
        total_rows, back.reshape(experts * slots, width), hidden, meta, meta_t, teacher, out_grad,
        valid[..., None], tiles, routes, experts, slots,
    )
    grads, _ = swap(sent, tile, n_z, True, 3)
    grad_x, d_in, d_back = expert_backward(
        core, grads.reshape(experts * slots, width), x, act, slope, w_in, w_back
    )
    home, _ = swap(grad_x.reshape(experts, slots, width), tile, n_z, True, 4)
    grad_images, dense = rear(
        home.reshape(experts * slots, width), images, hidden, grad_out, grad_logits, meta, proj, probs,
        mixed, weights, experts, n_z, n_g,
    )
    out_in, out_back, out_qkv, out_out, out_misc, loss = reduce_all(
        d_in, d_back, dense, square, count, n_z, n_g
    )
    return (
        loss[0, 0],
        output,
        grad_images,
        out_qkv,
        out_out,
        out_misc[:, experts],
        out_misc[:, experts + 1],
        out_misc[:, :experts],
        out_in,
        out_back,
    )


def solution(mesh):
    tokens = P(("dp", "expert"), None, None)
    in_specs = (
        tokens, tokens, tokens, P(("dp", "expert"), None), tokens,
        P("dp", None), P("dp", None), P("dp"), P("dp"), P("dp", None),
        P("expert", None, None), P("expert", None, None),
    )
    out_specs = (
        P(), tokens, tokens, P("dp", None), P("dp", None), P("dp"), P("dp"), P("dp", None),
        P("expert", "dp", None), P("expert", "dp", None),
    )
    return jax.shard_map(body, mesh=mesh, in_specs=in_specs, out_specs=out_specs, check_vma=False)
```

time: 634 us -> 286 us (0.45); the launches traced: 624 us -> 286 us
  Pallas kernels: 0 us -> 253 us
  blocking collectives: 171 us -> 0 us
  waiting for transfers between devices: 151 us -> 0 us
  matrix products: 90 us -> 0 us
  local copies, waits for them, and re-layouts: 114 us -> 29.5 us
  other arithmetic: 60.2 us -> 1.99 us
  between operations: 20.3 us -> 0.86 us
  starting transfers between devices: 18.4 us -> 0 us
    pallas_call x0 -> x11, Pallas kernels: none -> 253 us  [the longest x4 82.3 us: swap(): pl.pallas_call(functools.partial(swap_kernel, parts, n_z, plane), out_sha...]
    reduce_scatter x4 -> x0, waiting for transfers between devices: 95.8 us -> none  [the longest x1 36.4 us: body(): lax.psum_scatter(d_in_part.astype(jnp.bfloat16), 'dp', scatter_dimension=...]
    psum x3 -> x0, blocking collectives: 94.5 us -> none  [the longest x2 77.5 us: body(): count, sq_total = lax.psum((local_count, local_sq), ('dp', 'expert'))]
    dot_general x21 -> x0, matrix products: 90 us -> none  [the longest x1 30.4 us: body(): jnp.einsum('secd,edf->secf', arrived, w_in, preferred_element_type=jnp.fl...]
    gather x14 -> x0, local copies, waits for them, and re-layouts: 45.5 us -> none  [the longest x4 18.1 us: take_rows(): return jnp.take(padded, index, axis=0)]
    all_gather x3 -> x0, blocking collectives: 43.3 us -> none  [the longest x1 16 us: body(): lax.all_gather(w_qkv, 'dp', axis=0, tiled=True)]
    all_to_all x4 -> x0, waiting for transfers between devices: 40.2 us -> none  [the longest x1 16.9 us: body(): lax.all_to_all(grad_outgoing, 'expert', split_axis=0, concat_axis=0, tile...]
    unnamed x2 -> x0, blocking collectives: 32.7 us -> none
  transfers between devices with their start and end apart: 10 -> 0, of which waited for: 7 -> 0; matrix products, arithmetic and copies ran while one was open for 10% -> 0% of each run, Pallas kernels for 0% -> 0%
where the time goes in v1:
time: 286 us
  Pallas kernels  253 us (88%)
  local copies, waits for them, and re-layouts  29.5 us (10%)
    pallas_call x4, Pallas kernels, swap(): pl.pallas_call(functools.partial(swap_kernel, parts, n_z, plane), out_sha...  82.3 us
    pallas_call x1, Pallas kernels, reduce_all(): pl.pallas_call(functools.partial(reduce_kernel, n_z, n_g, width, parts),...  64.7 us
    unnamed x49, local copies, waits for them, and re-layouts  24.2 us
    pallas_call x1, Pallas kernels, gather_weights(): pl.pallas_call(functools.partial(gather_kernel, n_z), out_shape=jax.Shape...  20.9 us
    pallas_call x1, Pallas kernels, expert_backward(): pl.pallas_call(expert_back_kernel, grid_spec=pltpu.PrefetchScalarGridSpec...  18.3 us
    pallas_call x1, Pallas kernels, expert_forward(): pl.pallas_call(expert_kernel, grid_spec=pltpu.PrefetchScalarGridSpec(num_...  17.6 us
    pallas_call x1, Pallas kernels, rear(): pl.pallas_call(functools.partial(rear_kernel, experts, (n_z, blk, parts))...  17.3 us
    pallas_call x1, Pallas kernels, front(): pl.pallas_call(functools.partial(front_kernel, experts, slots), grid=(cou...  16.5 us

profile of v1, /device:TPU:0, one launch (start us, length us, event | category | flops | bytes accessed | tf_op | source)
XLA Modules:
  0.0 285.7 jit_solution(2016888296885386576)
XLA Ops:
  0.6 1.3 convert_reduce_fusion
  1.9 0.6 add.3.tile
  2.6 0.7 convert_bitcast_fusion
  3.3 0.8 copy.29
  4.0 0.8 copy.30
  4.8 0.8 copy.28
  5.6 1.0 concatenate.3.shard
  6.6 0.9 copy.32.refs_6_
  7.5 1.6 copy.31.routes.refs_8_
  9.0 20.9 %gather_weights.1 = bf16[8,48,1664]{2,1,0:T(8,128)(2,1)S(1)} custom-call(bf16[48,1664]{1,0:T(8,128)(2,1)S(1)} %concatenate.3.shard), custom_call_target="tpu_custom_call" | custom-call | tf_op jit(solution)/shard_map/gather_weights/pallas_call | solution.py:148
  29.9 0.0 copy-start
  29.9 1.1 copy-done
  31.0 16.5 %front.1 = (bf16[3,197,1152]{2,1,0:T(8,128)(2,1)}, f32[3,6,197,197]{3,2,1,0:T(8,128)}, bf16[3,197,384]{2,1,0:T(8,128)(2,1)}, f32[3,197,384]{2,1,0:T(8,128)}, f32...) custom-call(bf16[3,197,384]{2,1,0:T(8,128)(2,1)} %image.3, ...), custom_call_target="tpu_custom_call" | custom-call | tf_op jit(solution)/shard_map/front/pallas_call | solution.py:338
  47.5 0.0 copy-start.5
  47.5 1.4 copy-done.5
  48.9 20.7 %swap_1.1 = (bf16[8,240,384]{2,1,0:T(8,128)(2,1)S(1)}, f32[8,8,128]{2,1,0:T(8,128)S(1)}) custom-call(bf16[8,240,384]{2,1,0:T(8,128)(2,1)S(1)} %copy-done.5, f32[8,128]{1,0:T(8,128)S(1)} %add.3.tile), custom_call_target="tpu_custom_call" | custom-call | tf_op jit(solution)/shard_map/swap_1/pallas_call | solution.py:206
  69.6 1.1 copy-done.1
  70.7 0.6 copy-done.17
  71.3 17.6 %expert_forward.1 = (bf16[1920,1536]{1,0:T(8,128)(2,1)}, bf16[1920,1536]{1,0:T(8,128)(2,1)}, bf16[1920,384]{1,0:T(8,128)(2,1)}, f32[8,128]{1,0:T(8,128)}) custom-call(s32[1]{0:T(128)} %bitcast.core, bf16[1920,384]{1,0:T(8,128)(2,1)} %bitcast.19, bf16[2,384,1536]{2,1,0:T(8,128)(2,1)} %w_in.3, bf16[2,1536,384]{2,1,0:T(8,128)(2,1)} %w_back.3, ...), custom_call_target="tpu_custom_call" | custom-call | tf_op jit(solution)/shard_map/expert_forward/pallas_call | solution.py:408
  88.8 1.4 copy-done.7
  90.2 0.7 copy-done.15
  90.9 19.1 %swap_2.1 = (bf16[8,240,384]{2,1,0:T(8,128)(2,1)S(1)}, f32[4,8,128]{2,1,0:T(8,128)S(1)}) custom-call(bf16[8,240,384]{2,1,0:T(8,128)(2,1)S(1)} %bitcast.24, f32[8,128]{1,0:T(8,128)S(1)} %copy-done.15), custom_call_target="tpu_custom_call" | custom-call | tf_op jit(solution)/shard_map/swap_2/pallas_call | solution.py:206
  110.0 1.1 copy-done.8
  111.1 0.6 copy-done.18
  111.8 15.8 %middle.1 = (bf16[3,197,384]{2,1,0:T(8,128)(2,1)}, f32[3,197,384]{2,1,0:T(8,128)}, bf16[3,197,128]{2,1,0:T(8,128)(2,1)}, bf16[8,240,384]{2,1,0:T(8,128)(2,1)}, f32[8,128]{1,0:T(8,128)}, /*index=5*/f32[8,128]{1,0:T(8,128)}) custom-call(bf16[1920,384]{1,0:T(8,128)(2,1)} %bitcast.25, f32[3,197,384]{2,1,0:T(8,128)} %get-tuple-element.50.refs_1_.hidden, ...), custom_call_target="tpu_custom_call" | custom-call | tf_op jit(solution)/shard_map/middle/pallas_call | solution.py:518
  127.6 0.0 copy-done.16
  127.6 0.0 copy-start.3
  127.6 1.4 copy-done.3
  129.0 21.9 %swap_3.1 = (bf16[8,240,384]{2,1,0:T(8,128)(2,1)S(1)}, f32[8,8,128]{2,1,0:T(8,128)}) custom-call(bf16[8,240,384]{2,1,0:T(8,128)(2,1)S(1)} %copy-done.3, f32[8,128]{1,0:T(8,128)S(1)} %copy-done.16), custom_call_target="tpu_custom_call" | custom-call | tf_op jit(solution)/shard_map/swap_3/pallas_call | solution.py:206
  150.9 1.1 copy-done.6
  152.0 18.3 %expert_backward.1 = (bf16[1920,384]{1,0:T(8,128)(2,1)}, bf16[384,1536]{1,0:T(8,128)(2,1)}, bf16[1536,384]{1,0:T(8,128)(2,1)}) custom-call(s32[1]{0:T(128)} %bitcast.core, bf16[1920,384]{1,0:T(8,128)(2,1)} %bitcast.23, bf16[1920,384]{1,0:T(8,128)(2,1)} %bitcast.20, bf16[1920,1536]{1,0:T(8,128)(2,1)} %get-tuple-element.56.act, ...), custom_call_target="tpu_custom_call" | custom-call | tf_op jit(solution)/shard_map/expert_backward/pallas_call | solution.py:586
  170.3 1.4 copy-done.4
  171.7 20.6 %swap_4.1 = (bf16[8,240,384]{2,1,0:T(8,128)(2,1)S(1)}, f32[8,8,128]{2,1,0:T(8,128)}) custom-call(bf16[8,240,384]{2,1,0:T(8,128)(2,1)S(1)} %bitcast.22, f32[8,128]{1,0:T(8,128)S(1)} %copy-done.16), custom_call_target="tpu_custom_call" | custom-call | tf_op jit(solution)/shard_map/swap_4/pallas_call | solution.py:206
  192.3 1.1 copy-done.2
  193.5 17.3 %rear.1 = (bf16[3,197,384]{2,1,0:T(8,128)(2,1)}, bf16[2,4,4,24,896]{4,3,2,1,0:T(8,128)(2,1)}) custom-call(bf16[1920,384]{1,0:T(8,128)(2,1)} %bitcast.21, bf16[3,197,384]{2,1,0:T(8,128)(2,1)} %image.3, f32[3,197,384]{2,1,0:T(8,128)} %get-tuple-element.50.refs_1_.hidden, f32[3,197,384]{2,1,0:T(8,128)} %get-tuple-element.62.grad_out, ...), custom_call_target="tpu_custom_call" | custom-call | tf_op jit(solution)/shard_map/rear/pallas_call | solution.py:734
  210.8 1.3 copy-done.9
  212.1 64.7 %reduce_all.1 = (f32[2,48,1536]{2,1,0:T(8,128)S(1)}, f32[2,192,384]{2,1,0:T(8,128)S(1)}, f32[48,1152]{1,0:T(8,128)S(1)}, f32[48,384]{1,0:T(8,128)S(1)}, f32[48,128]{1,0:T(8,128)S(1)}, /*index=5*/f32[8,128]{1,0:T(8,128)S(1)}) custom-call(bf16[4,2,48,1536]{3,2,1,0:T(8,128)(2,1)S(1)} %bitcast.26, bf16[4,2,192,384]{3,2,1,0:T(8,128)(2,1)S(1)} %bitcast.27, ...), custom_call_target="tpu_custom_call" | custom-call | tf_op jit(solution)/shard_map/reduce_all/pallas_call | solution.py:891
  276.8 0.0 copy-start.12
  276.9 0.7 copy-done.12
  277.5 0.6 copy-done.14
  278.2 0.5 slice.12
  278.7 0.1 copy-done.13
  278.8 0.7 slice_reduce_fusion
  279.5 1.4 copy.34
  280.9 1.6 copy.39
  282.5 1.5 copy.40
  284.0 0.8 copy.41
  284.8 0.8 copy.42
  (22 shorter events, 0.0 us)
Async XLA Ops:
  29.9 1.1 copy-start
  47.5 1.4 copy-start.5
  69.6 1.1 copy-start.1
  70.7 0.6 copy-start.17
  88.8 1.4 copy-start.7
  90.2 0.7 copy-start.15
  110.0 1.1 copy-start.8
  111.1 0.6 copy-start.18
  111.7 15.8 %copy-start.16 = (f32[8,128]{1,0:T(8,128)S(1)}, f32[8,128]{1,0:T(8,128)}, u32[]{:S(2)}) copy-start(f32[8,128]{1,0:T(8,128)} %get-tuple-element.48.tile) | copy-start | bytes 12292
  127.6 1.4 copy-start.3
  150.9 1.1 copy-start.6
  170.3 1.4 copy-start.4
  192.3 1.1 copy-start.2
  193.5 17.3 %copy-start.10 = (bf16[384,1536]{1,0:T(8,128)(2,1)S(1)}, bf16[384,1536]{1,0:T(8,128)(2,1)}, u32[]{:S(2)}) copy-start(bf16[384,1536]{1,0:T(8,128)(2,1)} %get-tuple-element.58) | copy-start | bytes 3538948
  193.5 17.3 %copy-start.11 = (bf16[1536,384]{1,0:T(8,128)(2,1)S(1)}, bf16[1536,384]{1,0:T(8,128)(2,1)}, u32[]{:S(2)}) copy-start(bf16[1536,384]{1,0:T(8,128)(2,1)} %get-tuple-element.59) | copy-start | bytes 3538948
  193.5 17.3 %copy-start.19 = (f32[8,128]{1,0:T(8,128)S(1)}, f32[8,128]{1,0:T(8,128)}, u32[]{:S(2)}) copy-start(f32[8,128]{1,0:T(8,128)} %get-tuple-element.68.square) | copy-start | bytes 12292
  193.5 17.3 %copy-start.20 = (f32[8,128]{1,0:T(8,128)S(1)}, f32[8,128]{1,0:T(8,128)}, u32[]{:S(2)}) copy-start(f32[8,128]{1,0:T(8,128)} %get-tuple-element.69.count) | copy-start | bytes 12292
  210.8 1.3 copy-start.9
  276.8 0.7 copy-start.12
  277.5 0.6 copy-start.14
  278.2 0.6 copy-start.13

commit v2 on v1

--- a/solution.py
+++ b/solution.py
@@ -159,7 +159,7 @@
             pltpu.SemaphoreType.DMA((2,)),
         ],
         compiler_params=pltpu.CompilerParams(
-            collective_id=0, has_side_effects=True, vmem_limit_bytes=4 << 20
+            collective_id=0, has_side_effects=True
         ),
         name="gather_weights",
     )(shard).reshape(n_dp * rows, cols)
@@ -221,7 +221,7 @@
             pltpu.SemaphoreType.DMA((2,)),
         ],
         compiler_params=pltpu.CompilerParams(
-            collective_id=number, has_side_effects=True, vmem_limit_bytes=4 << 20
+            collective_id=number, has_side_effects=True
         ),
         name=f"swap_{number}",
     )(sent, tile)
@@ -623,56 +623,44 @@
     return row_parts, col_parts, rows // row_parts, tiles * LANES
 
 
-def rear_kernel(
-    experts, pieces, home, image, hidden, grad_out, grad_logits, meta, proj, probs, mixed, weights,
-    grad_image, dense, sum_qkv, sum_out, sum_misc, grad_proj,
+def rear_image(
+    i, experts, home, image, hidden, grad_out, grad_logits, meta, proj, probs, mixed, weights, gains,
+    router_t, grad_image, sum_qkv, sum_out, sum_misc, grad_proj,
 ):
-    step = pl.program_id(0)
     seq, width = image.shape[1:]
     heads = width // HEAD_DIM
-
-    @pl.when(step == 0)
-    def _():
-        sum_qkv[...] = jnp.zeros_like(sum_qkv)
-        sum_out[...] = jnp.zeros_like(sum_out)
-        sum_misc[...] = jnp.zeros_like(sum_misc)
-
-    w_qkv = weights[:, : 3 * width]
-    w_out = weights[:, 3 * width : 4 * width]
-    misc_t = weights[:, 4 * width :].astype(F32).T
-    gain_one = misc_t[experts : experts + 1]
-    gain_two = misc_t[experts + 1 : experts + 2]
-    places = [meta[0, :, 2 + k : 3 + k] for k in range(2)]
+    gain_one, gain_two = gains
+    places = [meta[i, :, 2 + k : 3 + k] for k in range(2)]
     all_slots = home.shape[0]
     chunk = chunk_of(all_slots)
-    logit_rows = grad_logits[0]
-    grad_two = mm(logit_rows, misc_t.astype(BF16))
+    logit_rows = grad_logits[i]
+    grad_two = mm(logit_rows, router_t)
     for n in range(all_slots // chunk):
         at = (iota((seq, chunk), 1) + n * chunk).astype(F32)
         pick = jnp.where((at == places[0]) | (at == places[1]), 1.0, 0.0).astype(BF16)
         grad_two += mm(pick, home[n * chunk : (n + 1) * chunk])
-    hhat, h_rstd = norm_stats(hidden[0])
+    hhat, h_rstd = norm_stats(hidden[i])
     normed_two = (hhat * gain_two).astype(BF16)
     d_gain_two = jnp.sum(grad_two * hhat, axis=0, keepdims=True)
-    grad_hidden = grad_out[0] + norm_back(grad_two, hhat, h_rstd, gain_two)
+    grad_hidden = grad_out[i] + norm_back(grad_two, hhat, h_rstd, gain_two)
     grad_attn = grad_hidden.astype(BF16)
-    sum_out[...] += mm_tn(mixed[0], grad_attn)
-    grad_mixed = mm_nt(grad_attn, w_out).astype(BF16)
+    sum_out[...] += mm_tn(mixed[i], grad_attn)
+    grad_mixed = mm_nt(grad_attn, weights[:, 3 * width : 4 * width]).astype(BF16)
     d_router = mm_tn(logit_rows, normed_two)
 
     scale = HEAD_DIM ** (-0.5)
     lower = iota((seq, LANES), 1) < HEAD_DIM
     for pair in range(heads // 2):
         at = pair * LANES
-        query = proj[0, :, at : at + LANES]
-        keys = proj[0, :, width + at : width + at + LANES]
-        values = proj[0, :, 2 * width + at : 2 * width + at + LANES]
+        query = proj[i, :, at : at + LANES]
+        keys = proj[i, :, width + at : width + at + LANES]
+        values = proj[i, :, 2 * width + at : 2 * width + at + LANES]
         grad_pair = grad_mixed[:, at : at + LANES]
         got = []
         for half in range(2):
             mask = lower if half == 0 else jnp.logical_not(lower)
             part = jnp.where(mask, grad_pair, jnp.zeros_like(grad_pair))
-            prob = probs[0, 2 * pair + half]
+            prob = probs[i, 2 * pair + half]
             grad_probs = mm_nt(part, values)
             inner = jnp.sum(grad_probs * prob, axis=-1, keepdims=True)
             grad_scores = (prob * (grad_probs - inner)).astype(BF16)
@@ -686,132 +674,121 @@
         for which in range(3):
             start = which * width + at
             grad_proj[:, start : start + LANES] = jnp.where(lower, got[0][which], got[1][which]).astype(BF16)
-    xhat, x_rstd = norm_stats(image[0].astype(F32))
+    xhat, x_rstd = norm_stats(image[i].astype(F32))
     normed_one = (xhat * gain_one).astype(BF16)
     sum_qkv[...] += mm_tn(normed_one, grad_proj[...])
-    grad_one = mm_nt(grad_proj[...], w_qkv)
+    grad_one = mm_nt(grad_proj[...], weights[:, : 3 * width])
     d_gain_one = jnp.sum(grad_one * xhat, axis=0, keepdims=True)
-    grad_image[0] = (grad_hidden + norm_back(grad_one, xhat, x_rstd, gain_one)).astype(BF16)
+    grad_image[i] = (grad_hidden + norm_back(grad_one, xhat, x_rstd, gain_one)).astype(BF16)
     row = iota((LANES, width), 0)
     sum_misc[...] += jnp.where(
         row == experts, d_gain_one, jnp.where(row == experts + 1, d_gain_two, d_router)
     )
 
-    @pl.when(step == pl.num_programs(0) - 1)
-    def _():
-        n_z, blk, (row_parts, col_parts, rows, cols) = pieces
-        misc = sum_misc[...].T
-        for z in range(n_z):
-            for c in range(CORES):
-                for r in range(row_parts):
-                    top = (z * CORES + c) * blk + r * rows
-                    for tile in range(col_parts * cols // LANES):
-                        left = tile * LANES
-                        q, inside = left // cols, left % cols
-                        if left < 3 * width:
-                            value = sum_qkv[top : top + rows, left : left + LANES]
-                        elif left < 4 * width:
-                            value = sum_out[top : top + rows, left - 3 * width : left - 3 * width + LANES]
-                        elif left == 4 * width:
-                            value = misc[top : top + rows]
-                        else:
-                            value = jnp.zeros((rows, LANES), F32)
-                        dense[c, r * col_parts + q, z, :, inside : inside + LANES] = value.astype(BF16)
-
-
-def rear(home, images, hidden, grad_out, grad_logits, meta, proj, probs, mixed, weights, experts, n_z, n_g):
-    count, seq, width = images.shape
-    blk = width // (n_z * CORES)
-    parts = piece_shape(n_g, blk, 4 * width + LANES)
-
-    def per_image(*shape):
-        return pl.BlockSpec((1, *shape), lambda i: (i,) + (0,) * len(shape))
-
-    def whole(*shape):
-        return pl.BlockSpec(shape, lambda i: (0,) * len(shape))
-
-    dense = (CORES, n_g, n_z, parts[2], parts[3])
-    return pl.pallas_call(
-        functools.partial(rear_kernel, experts, (n_z, blk, parts)),
-        grid=(count,),
-        out_shape=(
-            jax.ShapeDtypeStruct((count, seq, width), BF16),
-            jax.ShapeDtypeStruct(dense, BF16),
-        ),
-        in_specs=[
-            whole(*home.shape),
-            per_image(seq, width),
-            per_image(seq, width),
-            per_image(seq, width),
-            per_image(seq, LANES),
-            per_image(seq, LANES),
-            per_image(seq, 3 * width),
-            per_image(*probs.shape[1:]),
-            per_image(seq, width),
-            whole(*weights.shape),
-        ],
-        out_specs=(per_image(seq, width), whole(*dense)),
-        scratch_shapes=[
-            pltpu.VMEM((width, 3 * width), F32),
-            pltpu.VMEM((width, width), F32),
-            pltpu.VMEM((LANES, width), F32),
-            pltpu.VMEM((seq, 3 * width), BF16),
-        ],
-        name="rear",
-    )(home, images, hidden, grad_out, grad_logits, meta, proj, probs, mixed, weights)
-
-
-def reduce_kernel(
-    n_z, n_g, width, parts, d_in, d_back, dense, square, count,
-    out_in, out_back, out_qkv, out_out, out_misc, out_loss,
+
+def finish_kernel(
+    n_z, n_g, experts, slots, parts,
+    grad_x, image_h, hidden_h, grad_out_h, grad_logits_h, meta_h, proj_h, probs_h, mixed_h, weights_h,
+    d_in, d_back, square, count,
+    grad_image, out_in, out_back, out_qkv, out_out, out_misc, out_loss,
+    home, image, hidden, grad_out, grad_logits, meta, proj, probs, mixed, weights,
+    sum_qkv, sum_out, sum_misc, grad_proj, dense,
     own_in, own_back, got_in, got_back, give_in, give_back, take_in, take_back,
-    own_dense, got_dense, sum_dense, got_sum, own_piece, all_pieces, sq_plane, sq_give, sq_line,
-    s_exp, r_exp, s_core, r_core, s_a, r_a, s_b, r_b, s_c, r_c, s_q, r_q, s_l, r_l, local,
+    got_dense, sum_dense, got_sum, own_piece, all_pieces, sq_plane, sq_give, sq_line,
+    s_home, r_home, s_exp, r_exp, s_core, r_core, s_a, r_a, s_b, r_b, s_c, r_c, s_q, r_q, s_l, r_l, local,
 ):
     z, c, g = position()
     me = g * CORES + c
     members = n_g * CORES
     row_parts, col_parts, rows, cols = parts
+    count_images, seq, width = image.shape
     others = [lax.rem(me + k, members) for k in range(1, members)]
     plane = [device(z, lax.rem(e, CORES), e // CORES) for e in others]
     line_z = [lax.rem(z + k, n_z) for k in range(1, n_z)]
     line = [device(other, c, g) for other in line_z]
-    loads = [
-        pltpu.make_async_copy(d_in.at[z], own_in, local.at[0]),
-        pltpu.make_async_copy(d_back.at[z], own_back, local.at[1]),
-        pltpu.make_async_copy(dense.at[c, g], own_dense, local.at[2]),
-    ]
-    for load in loads:
-        load.start()
+
+    def slot_rows(e):
+        return pl.ds(pl.multiple_of(e * slots, 16), slots)
+
+    pairs = [
+        (grad_x.at[me], home.at[slot_rows(me)]),
+        (image_h, image), (hidden_h, hidden), (grad_out_h, grad_out), (grad_logits_h, grad_logits),
+        (meta_h, meta), (proj_h, proj), (probs_h, probs), (mixed_h, mixed), (weights_h, weights),
+        (d_in.at[z], own_in), (d_back.at[z], own_back),
+    ]
+    loads = [pltpu.make_async_copy(a, b, local.at[k]) for k, (a, b) in enumerate(pairs)]
     meet(plane + line)
+    swaps = [
+        remote(grad_x.at[e], home.at[slot_rows(me)], s_home.at[k], r_home.at[k], where)
+        for k, (e, where) in enumerate(zip(others, plane))
+    ]
+    step_q = [
+        remote(square, sq_plane.at[k], s_q.at[k], r_q.at[k], where) for k, where in enumerate(plane)
+    ]
+    heavy = []
+    for k, (other, where) in enumerate(zip(line_z, line)):
+        heavy.append(remote(d_in.at[other], got_in.at[k], s_exp.at[0, k], r_exp.at[0, k], where))
+        heavy.append(remote(d_back.at[other], got_back.at[k], s_exp.at[1, k], r_exp.at[1, k], where))
+    for copy in swaps + heavy + loads + step_q:
+        copy.start()
+    sum_qkv[...] = jnp.zeros_like(sum_qkv)
+    sum_out[...] = jnp.zeros_like(sum_out)
+    sum_misc[...] = jnp.zeros_like(sum_misc)
+    for copy in loads + step_q:
+        copy.wait()
+    misc_t = weights[:, 4 * width :].astype(F32).T
+    gains = (misc_t[experts : experts + 1], misc_t[experts + 1 : experts + 2])
+    router_t = misc_t.astype(BF16)
+    total = square[...]
+    for m in range(members - 1):
+        total += sq_plane[m]
+    sq_give[...] = total
+    for copy in swaps:
+        copy.wait()
+
+    def each(i, _):
+        rear_image(
+            i, experts, home, image, hidden, grad_out, grad_logits, meta, proj, probs, mixed, weights,
+            gains, router_t, grad_image, sum_qkv, sum_out, sum_misc, grad_proj,
+        )
+        return 0
+
+    lax.fori_loop(0, count_images, each, 0)
+
+    blk = rows * row_parts
+    misc = sum_misc[...].T
+    for zz in range(n_z):
+        for cc in range(CORES):
+            for r in range(row_parts):
+                top = (zz * CORES + cc) * blk + r * rows
+                for tile in range(col_parts * cols // LANES):
+                    left = tile * LANES
+                    q, inside = left // cols, left % cols
+                    if left < 3 * width:
+                        value = sum_qkv[top : top + rows, left : left + LANES]
+                    elif left < 4 * width:
+                        value = sum_out[top : top + rows, left - 3 * width : left - 3 * width + LANES]
+                    elif left == 4 * width:
+                        value = misc[top : top + rows]
+                    else:
+                        value = jnp.zeros((rows, LANES), F32)
+                    dense[cc, r * col_parts + q, zz, :, inside : inside + LANES] = value.astype(BF16)
+
     step_a = [
         remote(
             dense.at[lax.rem(e, CORES), e // CORES], got_dense.at[k], s_a.at[k], r_a.at[k], where
         )
         for k, (e, where) in enumerate(zip(others, plane))
     ]
-    step_q = [
-        remote(square, sq_plane.at[k], s_q.at[k], r_q.at[k], where) for k, where in enumerate(plane)
-    ]
-    heavy = []
-    for k, (other, where) in enumerate(zip(line_z, line)):
-        heavy.append(remote(d_in.at[other], got_in.at[k], s_exp.at[0, k], r_exp.at[0, k], where))
-        heavy.append(remote(d_back.at[other], got_back.at[k], s_exp.at[1, k], r_exp.at[1, k], where))
-    for copy in step_a + step_q + heavy:
+    for copy in step_a:
         copy.start()
-    for load in loads:
-        load.wait()
-    for copy in step_a + step_q:
+    for copy in step_a:
         copy.wait()
     for k in range(n_z):
-        total = own_dense[k].astype(F32)
+        total = dense[c, g, k].astype(F32)
         for m in range(members - 1):
             total += got_dense[m, k].astype(F32)
         sum_dense[k] = total.astype(BF16)
-    total = square[...]
-    for m in range(members - 1):
-        total += sq_plane[m]
-    sq_give[...] = total
     step_b = [
         remote(sum_dense.at[other], got_sum.at[k], s_b.at[k], r_b.at[k], where)
         for k, (other, where) in enumerate(zip(line_z, line))
@@ -821,6 +798,27 @@
     ]
     for copy in step_b + step_l:
         copy.start()
+
+    for copy in heavy:
+        copy.wait()
+    for own, got, give, out in ((own_in, got_in, give_in, out_in), (own_back, got_back, give_back, out_back)):
+
+        def total_of(half):
+            total = own[half].astype(F32)
+            for k in range(n_z - 1):
+                total += got[k, half].astype(F32)
+            return total
+
+        give[...] = total_of(1 - c).astype(BF16)
+        out[c] = total_of(c)
+    partner = device(z, 1 - c, g)
+    last = [
+        remote(give_in, take_in, s_core.at[0], r_core.at[0], partner),
+        remote(give_back, take_back, s_core.at[1], r_core.at[1], partner),
+    ]
+    for copy in last:
+        copy.start()
+
     for copy in step_b + step_l:
         copy.wait()
     total = sum_dense[z].astype(F32)
@@ -840,6 +838,10 @@
     for k in range(n_z - 1):
         total += sq_line[k]
     out_loss[...] = total / (count[...] * width)
+    for copy in last:
+        copy.wait()
+    out_in[1 - c] = take_in[...].astype(F32)
+    out_back[1 - c] = take_back[...].astype(F32)
     for copy in step_c:
         copy.wait()
     for r in range(row_parts):
@@ -855,42 +857,23 @@
             else:
                 out_misc[span, :] = value
 
-    for copy in heavy:
-        copy.wait()
-    for own, got, give, out in ((own_in, got_in, give_in, out_in), (own_back, got_back, give_back, out_back)):
-
-        def total_of(half):
-            total = own[half].astype(F32)
-            for k in range(n_z - 1):
-                total += got[k, half].astype(F32)
-            return total
-
-        give[...] = total_of(1 - c).astype(BF16)
-        out[c] = total_of(c)
-    partner = device(z, 1 - c, g)
-    last = [
-        remote(give_in, take_in, s_core.at[0], r_core.at[0], partner),
-        remote(give_back, take_back, s_core.at[1], r_core.at[1], partner),
-    ]
-    for copy in last:
-        copy.start()
-    for copy in last:
-        copy.wait()
-    out_in[1 - c] = take_in[...].astype(F32)
-    out_back[1 - c] = take_back[...].astype(F32)
-
-
-def reduce_all(d_in, d_back, dense, square, count, n_z, n_g):
+
+def finish(grad_x, saved, d_in, d_back, square, count, experts, n_z, n_g):
+    images = saved[0]
     width, hidden = d_in.shape
+    seq = images.shape[1]
+    slots = grad_x.shape[1]
     blk_in = width // (n_z * CORES)
     blk_back = hidden // (n_z * CORES)
     parts = piece_shape(n_g, blk_in, 4 * width + LANES)
     members = n_g * CORES
-    piece = dense.shape[-2:]
+    piece = parts[2:]
     dma = pltpu.SemaphoreType.DMA
+    both = lambda n: [dma((n,)), dma((n,))]
     return pl.pallas_call(
-        functools.partial(reduce_kernel, n_z, n_g, width, parts),
+        functools.partial(finish_kernel, n_z, n_g, experts, slots, parts),
         out_shape=(
+            jax.ShapeDtypeStruct(images.shape, BF16),
             jax.ShapeDtypeStruct((CORES, blk_in, hidden), F32),
             jax.ShapeDtypeStruct((CORES, blk_back, width), F32),
             jax.ShapeDtypeStruct((blk_in, 3 * width), F32),
@@ -898,9 +881,16 @@
             jax.ShapeDtypeStruct((blk_in, LANES), F32),
             jax.ShapeDtypeStruct((8, LANES), F32),
         ),
-        in_specs=[ANY, ANY, ANY, VMEM, VMEM],
-        out_specs=(VMEM,) * 6,
+        in_specs=[ANY] * (3 + len(saved)) + [VMEM, VMEM],
+        out_specs=(VMEM,) * 7,
         scratch_shapes=[
+            pltpu.VMEM((experts * slots, width), BF16),
+            *[pltpu.VMEM(v.shape, v.dtype) for v in saved],
+            pltpu.VMEM((width, 3 * width), F32),
+            pltpu.VMEM((width, width), F32),
+            pltpu.VMEM((LANES, width), F32),
+            pltpu.VMEM((seq, 3 * width), BF16),
+            pltpu.VMEM((CORES, n_g, n_z, *piece), BF16),
             pltpu.VMEM((CORES, blk_in, hidden), BF16),
             pltpu.VMEM((CORES, blk_back, width), BF16),
             pltpu.VMEM((n_z - 1, CORES, blk_in, hidden), BF16),
@@ -909,7 +899,6 @@
             pltpu.VMEM((blk_back, width), BF16),
             pltpu.VMEM((blk_in, hidden), BF16),
             pltpu.VMEM((blk_back, width), BF16),
-            pltpu.VMEM((n_z, *piece), BF16),
             pltpu.VMEM((members - 1, n_z, *piece), BF16),
             pltpu.VMEM((n_z, *piece), BF16),
             pltpu.VMEM((n_z - 1, *piece), BF16),
@@ -918,30 +907,24 @@
             pltpu.VMEM((members - 1, 8, LANES), F32),
             pltpu.VMEM((8, LANES), F32),
             pltpu.VMEM((n_z - 1, 8, LANES), F32),
+            *both(members - 1),
             dma((2, n_z - 1)),
             dma((2, n_z - 1)),
-            dma((2,)),
-            dma((2,)),
-            dma((members - 1,)),
-            dma((members - 1,)),
-            dma((n_z - 1,)),
-            dma((n_z - 1,)),
-            dma((n_g - 1,)),
-            dma((n_g - 1,)),
-            dma((members - 1,)),
-            dma((members - 1,)),
-            dma((n_z - 1,)),
-            dma((n_z - 1,)),
-            dma((3,)),
+            *both(2),
+            *both(members - 1),
+            *both(n_z - 1),
+            *both(n_g - 1),
+            *both(members - 1),
+            *both(n_z - 1),
+            dma((3 + len(saved),)),
         ],
-        compiler_params=pltpu.CompilerParams(
-            collective_id=5, has_side_effects=True, vmem_limit_bytes=32 << 20
-        ),
-        name="reduce_all",
+        compiler_params=pltpu.CompilerParams(collective_id=5, has_side_effects=True),
+        name="finish",
     )(
+        grad_x,
+        *saved,
         d_in.reshape(n_z, CORES, blk_in, hidden),
         d_back.reshape(n_z, CORES, blk_back, width),
-        dense,
         square,
         count,
     )
@@ -986,13 +969,10 @@
     grad_x, d_in, d_back = expert_backward(
         core, grads.reshape(experts * slots, width), x, act, slope, w_in, w_back
     )
-    home, _ = swap(grad_x.reshape(experts, slots, width), tile, n_z, True, 4)
-    grad_images, dense = rear(
-        home.reshape(experts * slots, width), images, hidden, grad_out, grad_logits, meta, proj, probs,
-        mixed, weights, experts, n_z, n_g,
-    )
-    out_in, out_back, out_qkv, out_out, out_misc, loss = reduce_all(
-        d_in, d_back, dense, square, count, n_z, n_g
+    grad_images, out_in, out_back, out_qkv, out_out, out_misc, loss = finish(
+        grad_x.reshape(experts, slots, width),
+        (images, hidden, grad_out, grad_logits, meta, proj, probs, mixed, weights),
+        d_in, d_back, square, count, experts, n_z, n_g,
     )
     return (
         loss[0, 0],

time: 286 us -> 238 us (0.83)
  Pallas kernels: 253 us -> 217 us
  local copies, waits for them, and re-layouts: 29.5 us -> 17.6 us
    pallas_call x4 -> x3, Pallas kernels: 82.3 us -> 61.8 us  [swap(): pl.pallas_call(functools.partial(swap_kernel, parts, n_z, plane), out_sha...]
    pallas_call x2 -> x1, Pallas kernels: 82 us -> 65.1 us  [finish(): pl.pallas_call(functools.partial(finish_kernel, n_z, n_g, experts, slots,...]
    unnamed x49 -> x14, local copies, waits for them, and re-layouts: 24.2 us -> 9.49 us
where the time goes in v2:
time: 238 us; the launch traced here: 237 us
  Pallas kernels  217 us (91%)
  local copies, waits for them, and re-layouts  17.6 us (7%)
    pallas_call x1, Pallas kernels, finish(): pl.pallas_call(functools.partial(finish_kernel, n_z, n_g, experts, slots,...  65.1 us
    pallas_call x3, Pallas kernels, swap(): pl.pallas_call(functools.partial(swap_kernel, parts, n_z, plane), out_sha...  61.8 us
    pallas_call x1, Pallas kernels, gather_weights(): pl.pallas_call(functools.partial(gather_kernel, n_z), out_shape=jax.Shape...  21.7 us
    pallas_call x1, Pallas kernels, expert_backward(): pl.pallas_call(expert_back_kernel, grid_spec=pltpu.PrefetchScalarGridSpec...  18.3 us
    pallas_call x1, Pallas kernels, expert_forward(): pl.pallas_call(expert_kernel, grid_spec=pltpu.PrefetchScalarGridSpec(num_...  17.6 us
    pallas_call x1, Pallas kernels, front(): pl.pallas_call(functools.partial(front_kernel, experts, slots), grid=(cou...  16.5 us
    pallas_call x1, Pallas kernels, middle(): pl.pallas_call(body, grid=(count,), out_shape=(jax.ShapeDtypeStruct((coun...  15.9 us
    unnamed x14, local copies, waits for them, and re-layouts  9.49 us

profile of v2, /device:TPU:0, one launch (start us, length us, event | category | flops | bytes accessed | tf_op | source)
XLA Modules:
  0.0 237.2 jit_solution(9948527086110960796)
XLA Ops:
  0.6 1.3 convert_reduce_fusion
  1.9 1.2 add.3.tile
  3.2 0.7 convert_bitcast_fusion
  3.9 0.8 copy.29
  4.6 0.8 copy.30
  5.4 0.8 copy.28
  6.2 1.7 concatenate.3.shard
  7.8 0.9 copy.32.refs_6_
  8.7 1.6 copy.31.routes.refs_8_
  10.3 21.7 %gather_weights.1 = bf16[8,48,1664]{2,1,0:T(8,128)(2,1)} custom-call(bf16[48,1664]{1,0:T(8,128)(2,1)} %concatenate.3.shard), custom_call_target="tpu_custom_call" | custom-call | tf_op jit(solution)/shard_map/gather_weights/pallas_call | solution.py:148
  32.0 16.5 %front.1 = (bf16[3,197,1152]{2,1,0:T(8,128)(2,1)}, f32[3,6,197,197]{3,2,1,0:T(8,128)}, bf16[3,197,384]{2,1,0:T(8,128)(2,1)}, f32[3,197,384]{2,1,0:T(8,128)}, f32...) custom-call(bf16[3,197,384]{2,1,0:T(8,128)(2,1)} %image_h.1, ...), custom_call_target="tpu_custom_call" | custom-call | tf_op jit(solution)/shard_map/front/pallas_call | solution.py:338
  48.5 20.8 %swap_1.1 = (bf16[8,240,384]{2,1,0:T(8,128)(2,1)}, f32[8,8,128]{2,1,0:T(8,128)}) custom-call(bf16[8,240,384]{2,1,0:T(8,128)(2,1)} %get-tuple-element.42.sent, f32[8,128]{1,0:T(8,128)} %add.3.tile), custom_call_target="tpu_custom_call" | custom-call | tf_op jit(solution)/shard_map/swap_1/pallas_call | solution.py:206
  69.3 17.6 %expert_forward.1 = (bf16[1920,1536]{1,0:T(8,128)(2,1)}, bf16[1920,1536]{1,0:T(8,128)(2,1)}, bf16[1920,384]{1,0:T(8,128)(2,1)}, f32[8,128]{1,0:T(8,128)}) custom-call(s32[1]{0:T(128)} %bitcast.core, bf16[1920,384]{1,0:T(8,128)(2,1)} %bitcast.18, bf16[2,384,1536]{2,1,0:T(8,128)(2,1)} %w_in.3, bf16[2,1536,384]{2,1,0:T(8,128)(2,1)} %w_back.3, ...), custom_call_target="tpu_custom_call" | custom-call | tf_op jit(solution)/shard_map/expert_forward/pallas_call | solution.py:408
  86.9 19.1 %swap_2.1 = (bf16[8,240,384]{2,1,0:T(8,128)(2,1)}, f32[4,8,128]{2,1,0:T(8,128)}) custom-call(bf16[8,240,384]{2,1,0:T(8,128)(2,1)} %bitcast.22, f32[8,128]{1,0:T(8,128)} %get-tuple-element.46.tile), custom_call_target="tpu_custom_call" | custom-call | tf_op jit(solution)/shard_map/swap_2/pallas_call | solution.py:206
  106.1 15.9 %middle.1 = (bf16[3,197,384]{2,1,0:T(8,128)(2,1)}, f32[3,197,384]{2,1,0:T(8,128)}, bf16[3,197,128]{2,1,0:T(8,128)(2,1)}, bf16[8,240,384]{2,1,0:T(8,128)(2,1)}, f32[8,128]{1,0:T(8,128)}, /*index=5*/f32[8,128]{1,0:T(8,128)}) custom-call(bf16[1920,384]{1,0:T(8,128)(2,1)} %bitcast.23, f32[3,197,384]{2,1,0:T(8,128)} %get-tuple-element.48.refs_1_.hidden_h, ...), custom_call_target="tpu_custom_call" | custom-call | tf_op jit(solution)/shard_map/middle/pallas_call | solution.py:518
  121.9 21.9 %swap_3.1 = (bf16[8,240,384]{2,1,0:T(8,128)(2,1)}, f32[8,8,128]{2,1,0:T(8,128)}) custom-call(bf16[8,240,384]{2,1,0:T(8,128)(2,1)} %get-tuple-element.52.sent, f32[8,128]{1,0:T(8,128)} %get-tuple-element.46.tile), custom_call_target="tpu_custom_call" | custom-call | tf_op jit(solution)/shard_map/swap_3/pallas_call | solution.py:206
  143.9 18.3 %expert_backward.1 = (bf16[1920,384]{1,0:T(8,128)(2,1)}, bf16[384,1536]{1,0:T(8,128)(2,1)}, bf16[1536,384]{1,0:T(8,128)(2,1)}) custom-call(s32[1]{0:T(128)} %bitcast.core, bf16[1920,384]{1,0:T(8,128)(2,1)} %bitcast.21, bf16[1920,384]{1,0:T(8,128)(2,1)} %bitcast.19, bf16[1920,1536]{1,0:T(8,128)(2,1)} %get-tuple-element.54.act, ...), custom_call_target="tpu_custom_call" | custom-call | tf_op jit(solution)/shard_map/expert_backward/pallas_call | solution.py:586
  162.1 65.1 %finish.1 = (bf16[3,197,384]{2,1,0:T(8,128)(2,1)}, f32[2,48,1536]{2,1,0:T(8,128)}, f32[2,192,384]{2,1,0:T(8,128)}, f32[48,1152]{1,0:T(8,128)}, f32[48,384]{1,0:T...) custom-call(bf16[8,240,384]{2,1,0:T(8,128)(2,1)} %bitcast.20, bf16[3,197,384]{2,1,0:T(8,128)(2,1)} %image_h.1, ...), custom_call_target="tpu_custom_call" | custom-call | tf_op jit(solution)/shard_map/finish/pallas_call | solution.py:873
  227.3 0.0 copy-start.2
  227.3 0.0 copy-start.1
  227.3 0.0 copy-start
  227.3 1.3 slice.12
  228.6 1.5 slice_reduce_fusion
  230.1 1.4 copy.34
  231.5 1.8 copy.40
  233.3 1.6 copy.41
  235.0 0.0 copy-done.2
  235.0 0.6 copy.42
  235.6 0.0 copy-done.1
  235.6 0.8 copy.43
  236.4 0.0 copy-done
  236.4 0.8 copy.44
  (1 shorter events, 0.0 us)
Async XLA Ops:
  227.3 7.7 %copy-start.2 = (f32[48,384]{1,0:T(8,128)S(1)}, f32[48,384]{1,0:T(8,128)}, u32[]{:S(2)}) copy-start(f32[48,384]{1,0:T(8,128)} %get-tuple-element.110) | copy-start | bytes 221188
  227.3 8.3 %copy-start.1 = (f32[2,48,1536]{2,1,0:T(8,128)S(1)}, f32[2,48,1536]{2,1,0:T(8,128)}, u32[]{:S(2)}) copy-start(f32[2,48,1536]{2,1,0:T(8,128)} %get-tuple-element.114) | copy-start | bytes 1769476
  227.3 9.1 %copy-start = (f32[2,192,384]{2,1,0:T(8,128)S(1)}, f32[2,192,384]{2,1,0:T(8,128)}, u32[]{:S(2)}) copy-start(f32[2,192,384]{2,1,0:T(8,128)} %get-tuple-element.115) | copy-start | bytes 1769476
